TPU v7x, 32 devices: a whole 2x2x4 slice. The times are simulated.
32 devices in a mesh: lat: 8 (over z, y), lon: 4 (over x, core).
Axes of the slice: x: 2, y: 2, z: 4, core: 2. Of those that a mesh axis runs over, the one named last changes fastest.
Arguments:
- state_fields: float32 [5, 32, 64, 4096], P(None, None, 'lat', 'lon'), may hold values from -6 to 6
- stencil_weights: float32 [4, 32, 64, 4096], P(None, None, 'lat', 'lon'), may hold values from 0.02 to 0.22
- filter_mask: int32 [64], replicated, may hold values from 0 to 1, as said below
- cutoff_wave: int32 [64], replicated, may hold values from 0 to 255, as said below
Outputs:
- advanced: float32 [5, 32, 64, 4096], P(None, None, 'lat', 'lon')
Inputs may be any that keep to these rules, and one draw needn't show every extreme that they name: `filter_mask`: every row outside the first and last 8 rows holds 0. `cutoff_wave`: from 1 to 255 in the first and last 8 rows, 0 elsewhere.
All inputs are finite; a program needn't handle non-finite values.
Results may differ from a plain program's by a relative error of at most 0.0011.
Values may be sent and summed in bfloat16 or wider, within the bound.
A program may use at most 64 MiB of HBM per device.

v0:
```python
import math

import jax
import jax.numpy as jnp
from jax import lax
from jax.sharding import PartitionSpec as P

NLON = 4096
KC = 256


def from_partner(block, axis, bit):
    count = lax.axis_size(axis)
    route = []
    for low in range(count):
        high = low | 1 << bit
        if high != low and high < count:
            route += [(low, high), (high, low)]
    return lax.ppermute(block, axis, route)


def with_halo(cells, sides, width, closed):
    for axis, dim in sides:
        count = lax.axis_size(axis)
        ends = count if closed else count - 1
        head = lax.slice_in_dim(cells, 0, width, axis=dim)
        tail = lax.slice_in_dim(cells, cells.shape[dim] - width, cells.shape[dim], axis=dim)
        cells = jnp.concatenate(
            [
                lax.ppermute(tail, axis, [(i, (i + 1) % count) for i in range(ends)]),
                cells,
                lax.ppermute(head, axis, [((i + 1) % count, i) for i in range(ends)]),
            ],
            axis=dim,
        )
    return cells


def wave_table(columns, mode_count, circle_size):
    wavenums = jnp.arange(2 * mode_count, dtype=jnp.int32) % mode_count
    product = columns[:, None] * wavenums[None, :] % circle_size
    angles = product.astype(jnp.float32) * (2.0 * math.pi / circle_size)
    upper = jnp.arange(2 * mode_count, dtype=jnp.int32) < mode_count
    return jnp.where(upper[None, :], jnp.cos(angles), jnp.sin(angles)).astype(jnp.bfloat16)


def mode_scale(cutoffs, mode_count, circle_size):
    wavenums = jnp.arange(2 * mode_count, dtype=jnp.int32) % mode_count
    weights = jnp.where(wavenums == 0, 1.0 / circle_size, 2.0 / circle_size).astype(jnp.float32)
    return jnp.where(wavenums[None, :] <= cutoffs[:, None], weights[None, :], jnp.float32(0.0))


def synthesize(spectra, circle_table):
    return lax.dot_general(
        spectra, circle_table, (((1,), (1,)), ((), ())), preferred_element_type=jnp.float32
    )


def on_device(state_fields, stencil_weights, filter_mask, cutoff_wave):
    field_count, levels, row_count, column_count = state_fields.shape
    lat_count = lax.axis_size("lat")
    lon_count = lax.axis_size("lon")
    lat_pos = lax.axis_index("lat")
    lon_pos = lax.axis_index("lon")
    circle_size = NLON
    mode_count = KC
    wind_signs = jnp.where(jnp.arange(field_count) < 2, -1.0, 1.0).astype(jnp.float32)[
        :, None, None
    ]
    pole_edges = jnp.stack([state_fields[:, :, 0], state_fields[:, :, -1]])
    partner = from_partner(
        pole_edges.astype(jnp.bfloat16), "lon", lon_count.bit_length() - 2
    ).astype(pole_edges.dtype)
    rimmed = with_halo(state_fields, (("lat", 2),), 1, False)
    north_edge = jnp.where(lat_pos == 0, wind_signs * partner[0], rimmed[:, :, 0])
    south_edge = jnp.where(lat_pos == lat_count - 1, wind_signs * partner[1], rimmed[:, :, -1])
    north_side = jnp.concatenate([north_edge[:, :, None], rimmed[:, :, 1:row_count]], axis=2)
    south_side = jnp.concatenate([rimmed[:, :, 2 : row_count + 1], south_edge[:, :, None]], axis=2)
    widened = with_halo(state_fields, (("lon", 3),), 1, True)
    west_side = widened[..., :-2]
    east_side = widened[..., 2:]
    stepped = (
        state_fields
        + stencil_weights[0] * (east_side - state_fields)
        + stencil_weights[1] * (west_side - state_fields)
        + stencil_weights[2] * (north_side - state_fields)
        + stencil_weights[3] * (south_side - state_fields)
    )
    item_count = field_count * levels
    rounded = stepped.astype(jnp.bfloat16).reshape(item_count, row_count, column_count)
    first_row = lat_pos * row_count
    local_cut = lax.dynamic_slice_in_dim(cutoff_wave, first_row, row_count)
    local_mask = lax.dynamic_slice_in_dim(filter_mask, first_row, row_count)
    flat_rows = rounded.reshape(item_count * row_count, column_count)
    segment = lax.all_gather(flat_rows, "lon", axis=1, tiled=True)
    columns = jnp.arange(segment.shape[1], dtype=jnp.int32)
    spectra = jnp.dot(
        segment, wave_table(columns, mode_count, circle_size), preferred_element_type=jnp.float32
    )
    spectra = (
        spectra.reshape(item_count, row_count, 2 * mode_count)
        * mode_scale(local_cut, mode_count, circle_size)[None]
    )
    spectra = spectra.astype(jnp.bfloat16)
    own_columns = lon_pos * column_count + jnp.arange(column_count, dtype=jnp.int32)
    smooth = synthesize(
        spectra.reshape(-1, 2 * mode_count), wave_table(own_columns, mode_count, circle_size)
    )
    smooth = smooth.astype(jnp.bfloat16).reshape(item_count, row_count, column_count)
    smooth = smooth.reshape(field_count, levels, row_count, column_count).astype(jnp.float32)
    return jnp.where(local_mask[None, None, :, None] == 1, smooth, stepped)


def solution(mesh):
    return jax.shard_map(
        on_device,
        mesh=mesh,
        in_specs=(P(None, None, "lat", "lon"), P(None, None, "lat", "lon"), P(), P()),
        out_specs=P(None, None, "lat", "lon"),
        check_vma=False,
    )
```

profile of v0, /device:TPU:9, one launch (start us, length us, event | category | flops | bytes accessed | tf_op | source)
XLA Modules:
  0.0 195.7 jit_solution(15504302779881839657)
XLA Ops:
  6.5 0.0 all-gather.2.cloned.1.call-start
  6.5 5.5 %fusion.56 = (f32[5,32,1,1024]{3,2,1,0:T(1,128)S(1)}, f32[5,32,1,1024]{3,2,1,0:T(1,128)S(1)}) fusion(f32[5,32,8,1024]{3,2,1,0:T(8,128)} %param.4), kind=kLoop, calls=%fused_computation.84 | loop fusion | bytes 2621440 | tf_op jit(solution)/shard_map/slice | solution.py:70
  12.0 0.2 convert_bitcast_fusion
  12.2 0.9 pad_maximum_fusion.2
  13.2 1.2 collective-permute-start.2
  14.4 1.0 copy.23
  15.4 3.1 %collective-permute-start.3 = (f32[5,32,1,1024]{3,1,0,2:T(8,128)}, f32[5,32,1,1024]{3,1,0,2:T(8,128)}, u32[]{:S(2)}, u32[]{:S(2)}) collective-permute-start(f32[5,32,1,1024]{3,1,0,2:T(8,128)} %copy.23), channel_id=1, source_target_pairs={{0,4},{4,8},{8,12},{12,16},{16,20},{20,24},{24,28},{1,5},{5,9},{9,... | collective-permute-start | bytes 1966088 | tf_op jit(solution)/shard_map/ppermute | solution.py:30
  18.6 1.0 copy.22
  19.5 3.0 %collective-permute-start.4 = (f32[5,32,1,1024]{3,1,0,2:T(8,128)}, f32[5,32,1,1024]{3,1,0,2:T(8,128)}, u32[]{:S(2)}, u32[]{:S(2)}) collective-permute-start(f32[5,32,1,1024]{3,1,0,2:T(8,128)} %copy.22), channel_id=1, source_target_pairs={{4,0},{8,4},{12,8},{16,12},{20,16},{24,20},{28,24},{5,1},{9,5},{13... | collective-permute-start | bytes 1966088 | tf_op jit(solution)/shard_map/ppermute | solution.py:32
  22.6 1.5 fusion.54
  24.1 0.0 slice-start
  24.1 0.3 copy.20
  24.4 1.5 collective-permute-start
  26.0 0.3 copy.21
  26.3 0.0 slice-start.1
  26.3 0.3 collective-permute-start.1
  26.6 4.1 %slice_bitcast_fusion.3 = (f32[32,8,1024]{2,1,0:T(8,128)S(1)}, f32[32,8,1024]{2,1,0:T(8,128)S(1)}, f32[32,8,1024]{2,1,0:T(8,128)}, f32[32,8,1024]{2,1,0:T(8,128)}) fusion(f32[4,32,8,1024]{3,2,1,0:T(8,128)} %param.5), kind=kLoop, calls=%fused_computation.55 | loop fusion | bytes 8388608 | tf_op jit(solution)/shard_map/mul | solution.py:84
  30.7 0.0 slice-done
  30.7 0.0 slice-done.1
  30.7 5.4 %fusion.55 = (f32[5,32,7,1024]{3,2,1,0:T(8,128)}, f32[5,32,7,1024]{3,2,1,0:T(8,128)}) fusion(f32[5,32,8,1024]{3,2,1,0:T(8,128)S(1)} %bitcast.41), kind=kLoop, calls=%fused_computation.83 | loop fusion | bytes 18350080 | tf_op jit(solution)/shard_map/slice | solution.py:77
  36.1 0.0 copy-start.1
  36.1 0.0 collective-permute-done
  36.1 1.2 copy.13
  37.2 0.0 collective-permute-done.1
  37.2 1.2 copy.15
  38.4 0.0 copy-start
  38.4 0.0 copy-start.2
  38.4 0.0 copy-start.3
  38.4 0.0 copy-start.4
  38.4 0.0 collective-permute-done.2
  38.4 1.4 convert_element_type.32
  39.8 6.2 %collective-permute-done.3 = f32[5,32,1,1024]{3,1,0,2:T(8,128)} collective-permute-done((f32[5,32,1,1024]{3,1,0,2:T(8,128)}, f32[5,32,1,1024]{3,1,0,2:T(8,128)}, u32[]{:S(2)}, u32[]{:S(2)}) %collective-permute-start.3) | collective-permute-done | bytes 655392 | tf_op jit(solution)/shard_map/ppermute | solution.py:30
  46.0 3.2 %collective-permute-done.4 = f32[5,32,1,1024]{3,1,0,2:T(8,128)} collective-permute-done((f32[5,32,1,1024]{3,1,0,2:T(8,128)}, f32[5,32,1,1024]{3,1,0,2:T(8,128)}, u32[]{:S(2)}, u32[]{:S(2)}) %collective-permute-start.4) | collective-permute-done | bytes 655392 | tf_op jit(solution)/shard_map/ppermute | solution.py:32
  49.2 1.6 fusion.40
  50.8 1.5 copy.18
  52.4 0.7 copy.19
  53.0 0.0 copy-done.1
  53.1 0.0 copy-done
  53.1 0.0 copy-done.2
  53.1 0.0 copy-done.3
  53.1 0.0 copy-done.4
  53.1 0.0 copy-start.5
  53.1 0.0 copy-start.6
  53.1 11.6 %fusion.52 = (bf16[5,32,8,1024]{3,2,1,0:T(8,128)(2,1)}, f32[5,32,8,1024]{3,2,1,0:T(8,128)}) fusion(f32[5,32,8,1024]{3,2,1,0:T(8,128)} %param.4, f32[5,32,1,1024]{3,2,1,0:T(1,128)S(1)} %copy.19, f32[5,32,7,1024]{3,2,1,0:T(8,128)} %get-tuple-element.10, f32[32,8,1024]{2,1,0:T(8,128)S(1)} %copy-done.1, f32[5,32,7,1024]{3,2,1,0:T(8,128)S(1)} %copy-done, ...), kind=kLoop, calls=%fused_computation.81 | loop fusion | flops 22282240 | bytes 27797504 | tf_op jit(solution)/shard_map/convert_element_type | solution.py:90
  64.7 0.0 all-gather.2.cloned.1.call-update
  64.8 0.0 copy-done.5
  64.8 0.1 dynamic_slice.7
  64.8 0.0 copy-done.6
  64.8 0.1 dynamic-slice_compare_fusion
  64.9 0.1 compare_select_fusion
  65.0 9.8 %select_convert_fusion.16 = bf16[1024,512]{1,0:T(8,128)(2,1)} fusion(s32[512]{0:T(512)S(1)} %add_select_fusion.2, s32[1024]{0:T(1024)S(1)} %iota_add_fusion, pred[512]{0:T(512)(128)(4,1)S(1)} %iota_compare_fusion), kind=kLoop, calls=%fused_computation.44.clone.clone.2 | loop fusion | flops 8388608 | bytes 1055232 | tf_op jit(solution)/shard_map/dot_general | solution.py:54
  74.8 59.8 %all-gather.2.cloned.1.call-done = bf16[1280,4096]{1,0:T(8,128)(2,1)} async-done(((bf16[1280,1024]{1,0:T(8,128)(2,1)}), bf16[1280,4096]{1,0:T(8,128)(2,1)}) %all-gather.2.cloned.1.call-update) | async-done | bytes 10485776 | tf_op jit(solution)/shard_map/all_gather | solution.py:95
  134.6 48.0 %convolution_convert_fusion = bf16[1280,1024]{1,0:T(8,128)(2,1)S(1)} fusion(bf16[1280,4096]{1,0:T(8,128)(2,1)} %all-gather.2.cloned.1.call-done, s32[512]{0:T(512)S(1)} %add_select_fusion.2, pred[512]{0:T(512)(128)(4,1)S(1)} %iota_compare_fusion, f32[8,512]{1,0:T(8,128)S(1)} %compare_select_fusion, bf16[1024,512]{1,0:T(8,128)(2,1)} %select_convert_fusion.16), kind=kOutput, calls=%fused_computation.35 | convolution fusion | flops 6747062272 | bytes 14174720 | tf_op jit(solution)/shard_map/dot_general | solution.py:54
  182.6 6.3 %convert_select_fusion = f32[5,32,8,1024]{3,2,1,0:T(8,128)} fusion(f32[5,32,8,1024]{3,2,1,0:T(8,128)} %get-tuple-element.6, bf16[5,32,8,1024]{3,2,1,0:T(8,128)(2,1)S(1)} %bitcast.43, pred[8]{0:T(512)(128)(4,1)S(1)} %dynamic-slice_compare_fusion), kind=kLoop, calls=%fused_computation.24 | loop fusion | flops 2621440 | bytes 13107208 | tf_op jit(solution)/shard_map/jit(_where)/select_n | solution.py:111
  (6 shorter events, 0.0 us)
Async XLA Ops:
  6.5 128.1 %all-gather.2.cloned.1.call-start = ((), (), s32[]{:S(2)}) async-start(), calls=%async_computation | async-start | bytes 13107200 | tf_op jit(solution)/shard_map/all_gather | solution.py:95
  13.2 25.2 %collective-permute-start.2 = (bf16[2,5,32,1024]{3,2,1,0:T(8,128)(2,1)}, bf16[2,5,32,1024]{3,2,1,0:T(8,128)(2,1)}, u32[]{:S(2)}, u32[]{:S(2)}) collective-permute-start(bf16[2,5,32,1024]{3,2,1,0:T(8,128)(2,1)} %pad_maximum_fusion.2), channel_id=1, source_target_pairs={{0,2},{2,0},{1,3},{3,1},{4,6},{6,4},{5,7},{7,5},{8,10},{10,8},{9,1... | collective-permute-start | bytes 1966088 | tf_op jit(solution)/shard_map/ppermute | solution.py:19
  15.4 30.6 %collective-permute-start.3 = (f32[5,32,1,1024]{3,1,0,2:T(8,128)}, f32[5,32,1,1024]{3,1,0,2:T(8,128)}, u32[]{:S(2)}, u32[]{:S(2)}) collective-permute-start(f32[5,32,1,1024]{3,1,0,2:T(8,128)} %copy.23), channel_id=1, source_target_pairs={{0,4},{4,8},{8,12},{12,16},{16,20},{20,24},{24,28},{1,5},{5,9},{9,... | collective-permute-start | bytes 1966088 | tf_op jit(solution)/shard_map/ppermute | solution.py:30
  19.5 29.7 %collective-permute-start.4 = (f32[5,32,1,1024]{3,1,0,2:T(8,128)}, f32[5,32,1,1024]{3,1,0,2:T(8,128)}, u32[]{:S(2)}, u32[]{:S(2)}) collective-permute-start(f32[5,32,1,1024]{3,1,0,2:T(8,128)} %copy.22), channel_id=1, source_target_pairs={{4,0},{8,4},{12,8},{16,12},{20,16},{24,20},{28,24},{5,1},{9,5},{13... | collective-permute-start | bytes 1966088 | tf_op jit(solution)/shard_map/ppermute | solution.py:32
  24.1 6.6 %slice-start = ((s8[5242880]{0:T(1024)(128)(4,1)}), s8[1048576]{0:T(1024)(128)(4,1)S(1)}, s32[]{:S(2)}) async-start(s8[5242880]{0:T(1024)(128)(4,1)} %bitcast.40), calls=%async_computation.1 | async-start | bytes 2097152
  24.4 11.6 %collective-permute-start = (f32[5,32,8,1]{1,2,3,0:T(8,128)S(1)}, f32[5,32,8,1]{1,2,3,0:T(8,128)S(1)}, u32[]{:S(2)}, u32[]{:S(2)}) collective-permute-start(f32[5,32,8,1]{1,2,3,0:T(8,128)S(1)} %copy.20), channel_id=1, source_target_pairs={{1,0},{2,1},{3,2},{0,3},{5,4},{6,5},{7,6},{4,7},{9,8},{10,9},{11,1... | collective-permute-start | bytes 15368 | tf_op jit(solution)/shard_map/ppermute | solution.py:32
  26.3 4.4 %slice-start.1 = ((s8[5242880]{0:T(1024)(128)(4,1)}), s8[4194304]{0:T(1024)(128)(4,1)S(1)}, s32[]{:S(2)}) async-start(s8[5242880]{0:T(1024)(128)(4,1)} %bitcast.40), calls=%async_computation.2 | async-start | bytes 8388608
  26.3 10.9 %collective-permute-start.1 = (f32[5,32,8,1]{1,2,3,0:T(8,128)S(1)}, f32[5,32,8,1]{1,2,3,0:T(8,128)S(1)}, u32[]{:S(2)}, u32[]{:S(2)}) collective-permute-start(f32[5,32,8,1]{1,2,3,0:T(8,128)S(1)} %copy.21), channel_id=1, source_target_pairs={{0,1},{1,2},{2,3},{3,0},{4,5},{5,6},{6,7},{7,4},{8,9},{9,10},{10,1... | collective-permute-start | bytes 15368 | tf_op jit(solution)/shard_map/ppermute | solution.py:30
  36.1 17.0 %copy-start.1 = (f32[32,8,1024]{2,1,0:T(8,128)S(1)}, f32[32,8,1024]{2,1,0:T(8,128)}, u32[]{:S(2)}) copy-start(f32[32,8,1024]{2,1,0:T(8,128)} %get-tuple-element.15) | copy-start | bytes 3145732
  38.4 14.6 %copy-start = (f32[5,32,7,1024]{3,2,1,0:T(8,128)S(1)}, f32[5,32,7,1024]{3,2,1,0:T(8,128)}, u32[]{:S(2)}) copy-start(f32[5,32,7,1024]{3,2,1,0:T(8,128)} %get-tuple-element.9) | copy-start | bytes 13762564
  38.4 14.7 %copy-start.2 = (f32[32,8,1024]{2,1,0:T(8,128)S(1)}, f32[32,8,1024]{2,1,0:T(8,128)}, u32[]{:S(2)}) copy-start(f32[32,8,1024]{2,1,0:T(8,128)} %get-tuple-element.16) | copy-start | bytes 3145732
  38.4 14.7 %copy-start.3 = (f32[5,32,8,1]{3,2,1,0:T(8,128)S(1)}, f32[5,32,8,1]{3,2,1,0:T(8,128)}, u32[]{:S(2)}) copy-start(f32[5,32,8,1]{3,2,1,0:T(8,128)} %copy.13) | copy-start | bytes 15364
  38.4 14.7 %copy-start.4 = (f32[5,32,8,1]{3,2,1,0:T(8,128)S(1)}, f32[5,32,8,1]{3,2,1,0:T(8,128)}, u32[]{:S(2)}) copy-start(f32[5,32,8,1]{3,2,1,0:T(8,128)} %copy.15) | copy-start | bytes 15364
  53.1 11.7 %copy-start.5 = (s32[64]{0:T(128)S(1)}, s32[64]{0:T(128)}, u32[]{:S(2)}) copy-start(s32[64]{0:T(128)} %param.7) | copy-start | bytes 772
  53.1 11.7 %copy-start.6 = (s32[64]{0:T(128)S(1)}, s32[64]{0:T(128)}, u32[]{:S(2)}) copy-start(s32[64]{0:T(128)} %param.6) | copy-start | bytes 772
Sparse Core Ops, SparseCore 0:
  64.9 69.6 all-gather.1
where the time goes:
time: 197 us; the launch traced here: 196 us
  waiting for transfers between devices  69.2 us (35%)
  matrix products  48 us (24%)
  other arithmetic  31.7 us (16%)
  local copies, waits for them, and re-layouts  24 us (12%)
  between operations  13.6 us (7%)
  starting transfers between devices  9.17 us (5%)
    all_gather x1, waiting for transfers between devices, on_device(): segment = lax.all_gather(flat_rows, 'lon', axis=1, tiled=True)  59.8 us
    dot_general x1, matrix products, synthesize(): lax.dot_general(spectra, circle_table, (((1,), (1,)), ((), ())), preferre...  48 us
    convert_element_type x1, other arithmetic, on_device(): stepped.astype(jnp.bfloat16).reshape(item_count, row_count, column_count)  11.6 us
    dot_general x1, other arithmetic, synthesize(): lax.dot_general(spectra, circle_table, (((1,), (1,)), ((), ())), preferre...  9.77 us
    select_n x1, other arithmetic, on_device(): return jnp.where(local_mask[None, None, :, None] == 1, smooth, stepped)  6.26 us
    ppermute x2, waiting for transfers between devices, with_halo(): lax.ppermute(tail, axis, [(i, (i + 1) % count) for i in range(ends)])  6.22 us
    slice x1, local copies, waits for them, and re-layouts, on_device(): pole_edges = jnp.stack([state_fields[:, :, 0], state_fields[:, :, -1]])  5.49 us
    slice x1, local copies, waits for them, and re-layouts, on_device(): rimmed[:, :, 1:row_count]  5.4 us
  transfers between devices with their start and end apart: 6, of which 3 were waited for; matrix products, arithmetic and copies ran while one was open for 14% of the time, Pallas kernels for 0%

commit v1 on v0

v1 whole, which is shorter than its diff:
```python
import math

import jax
import jax.numpy as jnp
from jax import lax
from jax.sharding import PartitionSpec as P

KC = 256


def flip(block, axis, bit):
    count = lax.axis_size(axis)
    route = [(i, i ^ (1 << bit)) for i in range(count) if i ^ (1 << bit) < count]
    return lax.ppermute(block, axis, route)


def shift(block, axis, step, closed):
    count = lax.axis_size(axis)
    route = [(i, (i + step) % count) for i in range(count) if closed or 0 <= i + step < count]
    return lax.ppermute(block, axis, route)


def angle_parts(columns, circle_size):
    waves = jnp.arange(KC, dtype=jnp.int32)
    product = columns[:, None] * waves[None, :] % circle_size
    angles = product.astype(jnp.float32) * (2.0 * math.pi / circle_size)
    return jnp.cos(angles), jnp.sin(angles)


def wave_table(first, column_count, circle_size):
    fine = 32
    coarse = column_count // fine
    cos_c, sin_c = angle_parts(first + fine * jnp.arange(coarse, dtype=jnp.int32), circle_size)
    cos_f, sin_f = angle_parts(jnp.arange(fine, dtype=jnp.int32), circle_size)
    cos_c, sin_c = cos_c[:, None], sin_c[:, None]
    cos_f, sin_f = cos_f[None], sin_f[None]
    table = jnp.concatenate(
        [cos_c * cos_f - sin_c * sin_f, sin_c * cos_f + cos_c * sin_f], axis=2
    )
    return table.astype(jnp.bfloat16).reshape(column_count, 2 * KC)


def mode_scale(cutoffs, circle_size):
    waves = jnp.arange(2 * KC, dtype=jnp.int32) % KC
    weights = jnp.where(waves == 0, 1.0 / circle_size, 2.0 / circle_size).astype(jnp.float32)
    return jnp.where(waves[None, :] <= cutoffs[:, None], weights[None, :], jnp.float32(0.0))


def on_device(state_fields, stencil_weights, filter_mask, cutoff_wave):
    fields, levels, rows, columns = state_fields.shape
    lat_count, lon_count = lax.axis_size("lat"), lax.axis_size("lon")
    lat_pos, lon_pos = lax.axis_index("lat"), lax.axis_index("lon")
    circle_size = columns * lon_count
    bits = lon_count.bit_length() - 1
    first_row = state_fields[:, :, 0]
    last_row = state_fields[:, :, -1]
    signs = jnp.where(jnp.arange(fields) < 2, -1.0, 1.0).astype(jnp.float32)[:, None, None]
    pole_row = jnp.where(lat_pos == 0, first_row, last_row).astype(jnp.bfloat16)
    over_pole = signs * flip(pole_row, "lon", bits - 1).astype(jnp.float32)
    north_in = shift(last_row.astype(jnp.bfloat16), "lat", 1, False).astype(jnp.float32)
    south_in = shift(first_row.astype(jnp.bfloat16), "lat", -1, False).astype(jnp.float32)
    north_edge = jnp.where(lat_pos == 0, over_pole, north_in)
    south_edge = jnp.where(lat_pos == lat_count - 1, over_pole, south_in)
    west_in = shift(state_fields[..., -1], "lon", 1, True)
    east_in = shift(state_fields[..., 0], "lon", -1, True)
    north_side = jnp.concatenate([north_edge[:, :, None], state_fields[:, :, :-1]], axis=2)
    south_side = jnp.concatenate([state_fields[:, :, 1:], south_edge[:, :, None]], axis=2)
    west_side = jnp.concatenate([west_in[..., None], state_fields[..., :-1]], axis=3)
    east_side = jnp.concatenate([state_fields[..., 1:], east_in[..., None]], axis=3)
    stepped = (
        state_fields
        + stencil_weights[0] * (east_side - state_fields)
        + stencil_weights[1] * (west_side - state_fields)
        + stencil_weights[2] * (north_side - state_fields)
        + stencil_weights[3] * (south_side - state_fields)
    )
    items = fields * levels
    start = lat_pos * rows
    cuts = lax.dynamic_slice_in_dim(cutoff_wave, start, rows)
    mask = lax.dynamic_slice_in_dim(filter_mask, start, rows)
    table = wave_table(lon_pos * columns, columns, circle_size)
    rounded = stepped.astype(jnp.bfloat16).reshape(items * rows, columns)
    partial = jnp.dot(rounded, table, preferred_element_type=jnp.float32)
    halves = partial.reshape(2, items * rows // 2, 2 * KC)
    low = lon_pos % 2 == 0
    mine = jnp.where(low, halves[0], halves[1])
    total = mine + flip(jnp.where(low, halves[1], halves[0]), "lon", 0)
    for bit in range(1, bits):
        total = total + flip(total.astype(jnp.float16), "lon", bit).astype(jnp.float32)
    scale = mode_scale(cuts, circle_size)
    spectra = (total.reshape(-1, rows, 2 * KC) * scale[None]).astype(jnp.bfloat16)
    other = flip(spectra, "lon", 0)
    spectra = jnp.concatenate(
        [jnp.where(low, spectra, other), jnp.where(low, other, spectra)], axis=0
    ).reshape(-1, 2 * KC)
    smooth = lax.dot_general(
        spectra, table, (((1,), (1,)), ((), ())), preferred_element_type=jnp.float32
    )
    smooth = smooth.astype(jnp.bfloat16).reshape(fields, levels, rows, columns)
    return jnp.where(mask[None, None, :, None] == 1, smooth.astype(jnp.float32), stepped)


def solution(mesh):
    return jax.shard_map(
        on_device,
        mesh=mesh,
        in_specs=(P(None, None, "lat", "lon"), P(None, None, "lat", "lon"), P(), P()),
        out_specs=P(None, None, "lat", "lon"),
        check_vma=False,
    )
```

time: 197 us -> 91.1 us (0.46)
  waiting for transfers between devices: 69.2 us -> 19.8 us
  matrix products: 48 us -> 3.1 us
  between operations: 13.6 us -> 0.24 us
  other arithmetic: 31.7 us -> 22.8 us
  local copies, waits for them, and re-layouts: 24 us -> 32.6 us
  starting transfers between devices: 9.17 us -> 12.2 us
    all_gather x1 -> x0, waiting for transfers between devices: 59.8 us -> none  [on_device(): segment = lax.all_gather(flat_rows, 'lon', axis=1, tiled=True)]
    dot_general x1 -> x2, matrix products: 48 us -> 3.1 us  [the longest x1 1.56 us: on_device(): lax.dot_general(spectra, table, (((1,), (1,)), ((), ())), preferred_eleme...]
    slice x3 -> x4, local copies, waits for them, and re-layouts: 12.4 us -> 23.4 us  [the longest x1 10.7 us: on_device(): state_fields[:, :, :-1]]
    ppermute x5 -> x8, waiting for transfers between devices: 9.4 us -> 19.8 us  [the longest x4 19.8 us: flip(): return lax.ppermute(block, axis, route)]
    dot_general x1 -> x0, other arithmetic: 9.77 us -> none  [synthesize(): lax.dot_general(spectra, circle_table, (((1,), (1,)), ((), ())), preferre...]
    broadcast_in_dim x0 -> x4, local copies, waits for them, and re-layouts: none -> 5.15 us  [the longest x1 1.9 us: on_device(): west_in[..., None]]
    select_n x6 -> x7, other arithmetic: 7.96 us -> 4.02 us  [the longest x1 3.29 us: on_device(): jnp.where(mask[None, None, :, None] == 1, smooth.astype(jnp.float32), ste...]
    ppermute x5 -> x8, starting transfers between devices: 9.17 us -> 12.2 us  [the longest x4 7.82 us: shift(): return lax.ppermute(block, axis, route)]
  transfers between devices with their start and end apart: 6 -> 8, of which waited for: 3 -> 3; matrix products, arithmetic and copies ran while one was open for 14% -> 30% of each run, Pallas kernels for 0% -> 0%
where the time goes in v1:
time: 91.1 us; the launch traced here: 90.8 us
  local copies, waits for them, and re-layouts  32.6 us (36%)
  other arithmetic  22.8 us (25%)
  waiting for transfers between devices  19.8 us (22%)
  starting transfers between devices  12.2 us (13%)
  matrix products  3.1 us (3%)
    ppermute x4, waiting for transfers between devices, flip(): return lax.ppermute(block, axis, route)  19.8 us
    convert_element_type x1, other arithmetic, on_device(): rounded = stepped.astype(jnp.bfloat16).reshape(items * rows, columns)  13.6 us
    slice x1, local copies, waits for them, and re-layouts, on_device(): state_fields[:, :, :-1]  10.7 us
    ppermute x4, starting transfers between devices, shift(): return lax.ppermute(block, axis, route)  7.82 us
    slice x1, local copies, waits for them, and re-layouts, on_device(): state_fields[..., 1:]  5.63 us
    slice x1, local copies, waits for them, and re-layouts, on_device(): last_row = state_fields[:, :, -1]  5.51 us
    ppermute x4, starting transfers between devices, flip(): return lax.ppermute(block, axis, route)  4.42 us
    select_n x1, other arithmetic, on_device(): jnp.where(mask[None, None, :, None] == 1, smooth.astype(jnp.float32), ste...  3.29 us
  transfers between devices with their start and end apart: 8, of which 3 were waited for; matrix products, arithmetic and copies ran while one was open for 30% of the time, Pallas kernels for 0%

profile of v1, /device:TPU:9, one launch (start us, length us, event | category | flops | bytes accessed | tf_op | source)
XLA Modules:
  0.0 90.8 jit_solution(14628865269078007904)
XLA Ops:
  0.0 5.5 %fusion.42 = (bf16[5,32,1,1024]{3,2,1,0:T(2,128)(2,1)S(1)}, bf16[5,32,1,1024]{3,2,1,0:T(2,128)(2,1)S(1)}) fusion(f32[5,32,8,1024]{3,2,1,0:T(8,128)} %param.4), kind=kLoop, calls=%fused_computation.79 | loop fusion | bytes 1310720 | tf_op jit(solution)/shard_map/slice | solution.py:56
  5.5 1.2 %fusion.13 = (bf16[5,32,1024]{2,1,0:T(8,128)(2,1)}, bf16[5,32,1024]{2,1,0:T(8,128)(2,1)}, bf16[5,32,1024]{2,1,0:T(8,128)(2,1)}) fusion(bf16[5,32,1,1024]{3,2,1,0:T(2,128)(2,1)S(1)} %get-tuple-element.15, bf16[5,32,1,1024]{3,2,1,0:T(2,128)(2,1)S(1)} %get-tuple-element.16, pred[]{:T(512)S(6)} %eq.31), kind=kLoop, calls=%fused_computation.38 | loop fusion | flops 163840 | bytes 1638401 | tf_op jit(solution)/shard_map/convert_element_type | solution.py:60
  6.7 3.1 %collective-permute-start.3 = (bf16[5,32,1024]{2,1,0:T(8,128)(2,1)}, bf16[5,32,1024]{2,1,0:T(8,128)(2,1)S(1)}, u32[]{:S(2)}, u32[]{:S(2)}) collective-permute-start(bf16[5,32,1024]{2,1,0:T(8,128)(2,1)} %get-tuple-element.23), channel_id=1, source_target_pairs={{0,4},{4,8},{8,12},{12,16},{16,20},{20,24},{24,28},{1,5},{5,9},{9,... | collective-permute-start | bytes 983048 | tf_op jit(solution)/shard_map/ppermute | solution.py:20
  9.9 1.3 %collective-permute-start.2 = (bf16[5,32,1024]{2,1,0:T(8,128)(2,1)}, bf16[5,32,1024]{2,1,0:T(8,128)(2,1)}, u32[]{:S(2)}, u32[]{:S(2)}) collective-permute-start(bf16[5,32,1024]{2,1,0:T(8,128)(2,1)} %get-tuple-element.24), channel_id=1, source_target_pairs={{0,2},{1,3},{2,0},{3,1},{4,6},{5,7},{6,4},{7,5},{8,10},{9,11},{10,... | collective-permute-start | bytes 983048 | tf_op jit(solution)/shard_map/ppermute | solution.py:14
  11.1 3.0 %collective-permute-start.4 = (bf16[5,32,1024]{2,1,0:T(8,128)(2,1)}, bf16[5,32,1024]{2,1,0:T(8,128)(2,1)}, u32[]{:S(2)}, u32[]{:S(2)}) collective-permute-start(bf16[5,32,1024]{2,1,0:T(8,128)(2,1)} %get-tuple-element.25), channel_id=1, source_target_pairs={{4,0},{8,4},{12,8},{16,12},{20,16},{24,20},{28,24},{5,1},{9,5},{13... | collective-permute-start | bytes 983048 | tf_op jit(solution)/shard_map/ppermute | solution.py:20
  14.2 1.5 %fusion.40 = (f32[5,32,8,1]{3,2,1,0:T(8,128)S(1)}, f32[5,32,8,1]{3,2,1,0:T(8,128)S(1)}) fusion(f32[5,32,8,1024]{3,2,1,0:T(8,128)} %param.4), kind=kLoop, calls=%fused_computation.77 | loop fusion | bytes 20480 | tf_op jit(solution)/shard_map/slice | solution.py:65
  15.7 0.9 %copy.19 = f32[5,32,8,1]{1,2,0,3:T(8,128)} copy(f32[5,32,8,1]{3,2,1,0:T(8,128)S(1)} %get-tuple-element.12) | data formatting | bytes 10240
  16.6 1.7 %collective-permute-start.1 = (f32[5,32,8]{1,2,0:T(8,128)}, f32[5,32,8]{1,2,0:T(8,128)}, u32[]{:S(2)}, u32[]{:S(2)}) collective-permute-start(f32[5,32,8]{1,2,0:T(8,128)} %bitcast.4), channel_id=1, source_target_pairs={{0,1},{1,2},{2,3},{3,0},{4,5},{5,6},{6,7},{7,4},{8,9},{9,10},{10,1... | collective-permute-start | bytes 15368 | tf_op jit(solution)/shard_map/ppermute | solution.py:20
  18.3 0.0 slice-start
  18.3 0.9 %copy.18 = f32[5,32,8,1]{1,2,0,3:T(8,128)} copy(f32[5,32,8,1]{3,2,1,0:T(8,128)S(1)} %get-tuple-element.11) | data formatting | bytes 10240
  19.2 0.0 collective-permute-start
  19.2 10.7 %fusion.41 = (f32[5,32,7,1024]{3,2,1,0:T(8,128)}, f32[5,32,7,1024]{3,2,1,0:T(8,128)}) fusion(f32[5,32,8,1024]{3,2,1,0:T(8,128)} %param.4), kind=kLoop, calls=%fused_computation.78 | loop fusion | bytes 18350080 | tf_op jit(solution)/shard_map/slice | solution.py:66
  29.9 0.0 slice-done
  29.9 0.0 slice-done.1
  29.9 5.6 %fusion.39 = (f32[5,32,8,1023]{3,2,1,0:T(8,128)}, f32[5,32,8,1023]{3,2,1,0:T(8,128)}) fusion(f32[5,32,8,1024]{3,2,1,0:T(8,128)S(1)} %bitcast.38), kind=kLoop, calls=%fused_computation.76 | loop fusion | bytes 20951040 | tf_op jit(solution)/shard_map/slice | solution.py:69
  35.6 0.1 fusion.27
  35.7 0.0 copy-done
  35.7 1.5 %slice_bitcast_fusion.3 = (f32[32,8,1024]{2,1,0:T(8,128)S(1)}, f32[32,8,1024]{2,1,0:T(8,128)S(1)}, f32[32,8,1024]{2,1,0:T(8,128)S(1)}, f32[32,8,1024]{2,1,0:T(8,128)}) fusion(f32[4,32,8,1024]{3,2,1,0:T(8,128)S(1)} %copy-done), kind=kLoop, calls=%fused_computation.27 | loop fusion | bytes 8388608 | tf_op jit(solution)/shard_map/mul | solution.py:72
  37.2 0.2 fusion.30
  37.4 1.4 %subtract_convert_fusion = (bf16[32,32,256]{2,1,0:T(8,128)(2,1)}, bf16[32,32,256]{2,1,0:T(8,128)(2,1)}) fusion(f32[32,256]{1,0:T(8,128)S(1)} %get-tuple-element.32, f32[32,256]{1,0:T(8,128)S(1)} %get-tuple-element.31, f32[32,256]{1,0:T(8,128)S(1)} %get-tuple-element.33, f32[32,256]{1,0:T(8,128)S(1)} %get-tuple-element.30), kind=kLoop, calls=%fused_computation.23 | loop fusion | flops 2097152 | bytes 1179648 | tf_op jit(solution)/shard_map/convert.4
  38.8 0.0 collective-permute-done.1
  38.8 1.9 %copy.13 = f32[5,32,8,1]{3,2,1,0:T(8,128)} copy(f32[5,32,8,1]{1,2,3,0:T(8,128)} %bitcast.5) | data formatting | bytes 10240 | tf_op jit(solution)/shard_map/broadcast_in_dim | solution.py:68
  40.7 0.0 collective-permute-done
  40.7 1.9 %copy.11 = f32[5,32,8,1]{3,2,1,0:T(8,128)} copy(f32[5,32,8,1]{1,2,3,0:T(8,128)} %bitcast.2) | data formatting | bytes 10240 | tf_op jit(solution)/shard_map/broadcast_in_dim | solution.py:69
  42.6 0.0 collective-permute-done.3
  42.6 0.0 collective-permute-done.2
  42.6 0.0 collective-permute-done.4
  42.6 1.5 %select_bitcast_fusion.1 = (f32[5,32,1,1024]{3,1,0,2:T(8,128)S(1)}, f32[5,32,1,1024]{3,1,0,2:T(8,128)S(1)}) fusion(bf16[5,32,1024]{2,1,0:T(8,128)(2,1)S(1)} %collective-permute-done.3, bf16[5,32,1024]{2,1,0:T(8,128)(2,1)} %collective-permute-done.2, f32[5]{0:T(128)S(1)} %compare_select_fusion.2, pred[]{:T(512)S(6)} %eq.31, ...), kind=kLoop, calls=%fused_computation.30 | loop fusion | flops 983040 | bytes 2293782 | tf_op jit(solution)/shard_map/broadcast_in_dim | solution.py:66
  44.1 0.7 copy.17
  44.8 0.7 copy.16
  45.5 0.0 copy-done.1
  45.5 0.0 copy-done.2
  45.5 0.0 copy-done.3
  45.5 0.0 copy-start.4
  45.5 0.0 copy-start.6
  45.5 13.6 %fusion.37 = (bf16[5,32,8,1024]{3,2,1,0:T(8,128)(2,1)S(1)}, f32[5,32,8,1024]{3,2,1,0:T(8,128)}) fusion(f32[5,32,8,1024]{3,2,1,0:T(8,128)} %param.4, f32[5,32,1,1024]{3,2,1,0:T(1,128)S(1)} %copy.17, f32[5,32,7,1024]{3,2,1,0:T(8,128)} %get-tuple-element.14, f32[32,8,1024]{2,1,0:T(8,128)S(1)} %get-tuple-element.19, f32[5,32,7,1024]{3,2,1,0:T(8,128)} %get-tuple-element.13, ...), kind=kLoop, calls=%fused_computation.75 | loop fusion | flops 22282240 | bytes 38273024 | tf_op jit(solution)/shard_map/convert_element_type | solution.py:82
  59.1 0.0 copy-done.4
  59.1 0.0 copy-done.6
  59.1 1.5 %fusion.11 = f32[1280,512]{1,0:T(8,128)S(1)} fusion(bf16[1280,1024]{1,0:T(8,128)(2,1)S(1)} %bitcast.41, bf16[1024,256]{1,0:T(8,128)(2,1)S(1)} %bitcast.45, bf16[1024,256]{1,0:T(8,128)(2,1)S(1)} %bitcast.43), kind=kOutput, calls=%fused_computation.28 | convolution fusion | flops 1344274432 | bytes 6291456 | tf_op jit(solution)/shard_map/dot_general | solution.py:83
  60.7 0.0 copy-start.8
  60.7 0.3 slice_select_fusion
  61.0 0.0 copy-start.9
  61.0 0.0 copy-start.5
  61.0 1.5 %collective-permute-start.5 = (f32[640,512]{1,0:T(8,128)S(1)}, f32[640,512]{1,0:T(8,128)S(1)}, u32[]{:S(2)}, u32[]{:S(2)}) collective-permute-start(f32[640,512]{1,0:T(8,128)S(1)} %slice_select_fusion), channel_id=1, source_target_pairs={{0,1},{1,0},{2,3},{3,2},{4,5},{5,4},{6,7},{7,6},{8,9},{9,8},{10,11... | collective-permute-start | bytes 3932168 | tf_op jit(solution)/shard_map/ppermute | solution.py:14
  62.5 2.7 %collective-permute-done.5 = f32[640,512]{1,0:T(8,128)S(1)} collective-permute-done((f32[640,512]{1,0:T(8,128)S(1)}, f32[640,512]{1,0:T(8,128)S(1)}, u32[]{:S(2)}, u32[]{:S(2)}) %collective-permute-start.5) | collective-permute-done | bytes 1310752 | tf_op jit(solution)/shard_map/ppermute | solution.py:14
  65.2 0.5 fusion.36
  65.7 0.3 collective-permute-start.6
  66.0 0.0 copy-done.8
  66.0 0.1 dynamic_slice.7
  66.1 0.1 compare_select_fusion
  66.2 15.5 %collective-permute-done.6 = f16[640,512]{1,0:T(8,128)(2,1)S(1)} collective-permute-done((f16[640,512]{1,0:T(8,128)(2,1)S(1)}, f16[640,512]{1,0:T(8,128)(2,1)S(1)}, u32[]{:S(2)}, u32[]{:S(2)}) %collective-permute-start.6) | collective-permute-done | bytes 655392 | tf_op jit(solution)/shard_map/ppermute | solution.py:14
  81.7 0.2 fusion.10
  81.9 1.3 %collective-permute-start.7 = (bf16[80,8,512]{2,1,0:T(8,128)(2,1)S(1)}, bf16[80,8,512]{2,1,0:T(8,128)(2,1)S(1)}, u32[]{:S(2)}, u32[]{:S(2)}) collective-permute-start(bf16[80,8,512]{2,1,0:T(8,128)(2,1)S(1)} %fusion.10), channel_id=1, source_target_pairs={{0,1},{1,0},{2,3},{3,2},{4,5},{5,4},{6,7},{7,6},{8,9},{9,8},{10,11... | collective-permute-start | bytes 1966088 | tf_op jit(solution)/shard_map/ppermute | solution.py:14
  83.2 0.0 copy-done.9
  83.2 0.1 dynamic-slice_compare_fusion
  83.3 1.6 %collective-permute-done.7 = bf16[80,8,512]{2,1,0:T(8,128)(2,1)S(1)} collective-permute-done((bf16[80,8,512]{2,1,0:T(8,128)(2,1)S(1)}, bf16[80,8,512]{2,1,0:T(8,128)(2,1)S(1)}, u32[]{:S(2)}, u32[]{:S(2)}) %collective-permute-start.7) | collective-permute-done | bytes 655392 | tf_op jit(solution)/shard_map/ppermute | solution.py:14
  84.9 0.4 broadcast_select_fusion.1
  85.3 0.0 copy-done.5
  85.3 0.0 copy-done.7
  85.3 0.0 slice-start.3
  85.3 1.6 %convolution_convert_fusion = bf16[1280,1024]{1,0:T(8,128)(2,1)S(1)} fusion(bf16[80,8,512]{2,1,0:T(8,128)(2,1)S(1)} %get-tuple-element.22, bf16[80,8,512]{2,1,0:T(8,128)(2,1)S(1)} %get-tuple-element.21, bf16[1024,256]{1,0:T(8,128)(2,1)S(1)} %bitcast.46, bf16[1024,256]{1,0:T(8,128)(2,1)S(1)} %bitcast.44), kind=kOutput, calls=%fused_computation.13 | convolution fusion | flops 1346240512 | bytes 4980736 | tf_op jit(solution)/shard_map/dot_general | solution.py:96
  86.9 0.2 slice-done.2
  87.1 0.4 slice-done.3
  87.5 3.3 %convert_select_fusion = f32[5,32,8,1024]{3,2,1,0:T(8,128)} fusion(f32[5,32,8,1024]{3,2,1,0:T(8,128)S(1)} %bitcast.40, bf16[5,32,8,1024]{3,2,1,0:T(8,128)(2,1)S(1)} %bitcast.42, pred[8]{0:T(512)(128)(4,1)S(1)} %dynamic-slice_compare_fusion), kind=kLoop, calls=%fused_computation.12 | loop fusion | flops 2621440 | bytes 13107208 | tf_op jit(solution)/shard_map/jit(_where)/select_n | solution.py:100
  (13 shorter events, 0.0 us)
Async XLA Ops:
  6.7 35.9 %collective-permute-start.3 = (bf16[5,32,1024]{2,1,0:T(8,128)(2,1)}, bf16[5,32,1024]{2,1,0:T(8,128)(2,1)S(1)}, u32[]{:S(2)}, u32[]{:S(2)}) collective-permute-start(bf16[5,32,1024]{2,1,0:T(8,128)(2,1)} %get-tuple-element.23), channel_id=1, source_target_pairs={{0,4},{4,8},{8,12},{12,16},{16,20},{20,24},{24,28},{1,5},{5,9},{9,... | collective-permute-start | bytes 983048 | tf_op jit(solution)/shard_map/ppermute | solution.py:20
  9.9 32.8 %collective-permute-start.2 = (bf16[5,32,1024]{2,1,0:T(8,128)(2,1)}, bf16[5,32,1024]{2,1,0:T(8,128)(2,1)}, u32[]{:S(2)}, u32[]{:S(2)}) collective-permute-start(bf16[5,32,1024]{2,1,0:T(8,128)(2,1)} %get-tuple-element.24), channel_id=1, source_target_pairs={{0,2},{1,3},{2,0},{3,1},{4,6},{5,7},{6,4},{7,5},{8,10},{9,11},{10,... | collective-permute-start | bytes 983048 | tf_op jit(solution)/shard_map/ppermute | solution.py:14
  11.1 31.5 %collective-permute-start.4 = (bf16[5,32,1024]{2,1,0:T(8,128)(2,1)}, bf16[5,32,1024]{2,1,0:T(8,128)(2,1)}, u32[]{:S(2)}, u32[]{:S(2)}) collective-permute-start(bf16[5,32,1024]{2,1,0:T(8,128)(2,1)} %get-tuple-element.25), channel_id=1, source_target_pairs={{4,0},{8,4},{12,8},{16,12},{20,16},{24,20},{28,24},{5,1},{9,5},{13... | collective-permute-start | bytes 983048 | tf_op jit(solution)/shard_map/ppermute | solution.py:20
  16.6 22.2 %collective-permute-start.1 = (f32[5,32,8]{1,2,0:T(8,128)}, f32[5,32,8]{1,2,0:T(8,128)}, u32[]{:S(2)}, u32[]{:S(2)}) collective-permute-start(f32[5,32,8]{1,2,0:T(8,128)} %bitcast.4), channel_id=1, source_target_pairs={{0,1},{1,2},{2,3},{3,0},{4,5},{5,6},{6,7},{7,4},{8,9},{9,10},{10,1... | collective-permute-start | bytes 15368 | tf_op jit(solution)/shard_map/ppermute | solution.py:20
  18.3 11.6 %slice-start = ((s8[5242880]{0:T(1024)(128)(4,1)}), s8[1048576]{0:T(1024)(128)(4,1)S(1)}, s32[]{:S(2)}) async-start(s8[5242880]{0:T(1024)(128)(4,1)} %bitcast.37), calls=%async_computation | async-start | bytes 2097152
  19.2 10.7 %slice-start.1 = ((s8[5242880]{0:T(1024)(128)(4,1)}), s8[4194304]{0:T(1024)(128)(4,1)S(1)}, s32[]{:S(2)}) async-start(s8[5242880]{0:T(1024)(128)(4,1)} %bitcast.37), calls=%async_computation.1 | async-start | bytes 8388608
  19.2 21.5 %collective-permute-start = (f32[5,32,8]{1,2,0:T(8,128)}, f32[5,32,8]{1,2,0:T(8,128)}, u32[]{:S(2)}, u32[]{:S(2)}) collective-permute-start(f32[5,32,8]{1,2,0:T(8,128)} %bitcast.1), channel_id=1, source_target_pairs={{0,3},{1,0},{2,1},{3,2},{4,7},{5,4},{6,5},{7,6},{8,11},{9,8},{10,9... | collective-permute-start | bytes 15368 | tf_op jit(solution)/shard_map/ppermute | solution.py:20
  29.9 5.8 %copy-start = (f32[4,32,8,1024]{3,2,1,0:T(8,128)S(1)}, f32[4,32,8,1024]{3,2,1,0:T(8,128)}, u32[]{:S(2)}) copy-start(f32[4,32,8,1024]{3,2,1,0:T(8,128)} %param.5) | copy-start | bytes 12582916
  42.6 2.9 %copy-start.1 = (f32[32,8,1024]{2,1,0:T(8,128)S(1)}, f32[32,8,1024]{2,1,0:T(8,128)}, u32[]{:S(2)}) copy-start(f32[32,8,1024]{2,1,0:T(8,128)} %get-tuple-element.20) | copy-start | bytes 3145732
  42.6 2.9 %copy-start.2 = (f32[5,32,8,1]{3,2,1,0:T(8,128)S(1)}, f32[5,32,8,1]{3,2,1,0:T(8,128)}, u32[]{:S(2)}) copy-start(f32[5,32,8,1]{3,2,1,0:T(8,128)} %copy.13) | copy-start | bytes 15364
  42.6 2.9 %copy-start.3 = (f32[5,32,8,1]{3,2,1,0:T(8,128)S(1)}, f32[5,32,8,1]{3,2,1,0:T(8,128)}, u32[]{:S(2)}) copy-start(f32[5,32,8,1]{3,2,1,0:T(8,128)} %copy.11) | copy-start | bytes 15364
  45.5 13.6 %copy-start.4 = (bf16[32,32,256]{2,1,0:T(8,128)(2,1)S(1)}, bf16[32,32,256]{2,1,0:T(8,128)(2,1)}, u32[]{:S(2)}) copy-start(bf16[32,32,256]{2,1,0:T(8,128)(2,1)} %get-tuple-element.28) | copy-start | bytes 1572868
  45.5 13.6 %copy-start.6 = (bf16[32,32,256]{2,1,0:T(8,128)(2,1)S(1)}, bf16[32,32,256]{2,1,0:T(8,128)(2,1)}, u32[]{:S(2)}) copy-start(bf16[32,32,256]{2,1,0:T(8,128)(2,1)} %get-tuple-element.29) | copy-start | bytes 1572868
  60.7 5.3 %copy-start.8 = (s32[64]{0:T(128)S(1)}, s32[64]{0:T(128)}, u32[]{:S(2)}) copy-start(s32[64]{0:T(128)} %param.7) | copy-start | bytes 772
  61.0 22.2 %copy-start.9 = (s32[64]{0:T(128)S(1)}, s32[64]{0:T(128)}, u32[]{:S(2)}) copy-start(s32[64]{0:T(128)} %param.6) | copy-start | bytes 772
  61.0 24.3 %copy-start.5 = (bf16[32,32,256]{2,1,0:T(8,128)(2,1)S(1)}, bf16[32,32,256]{2,1,0:T(8,128)(2,1)}, u32[]{:S(2)}) copy-start(bf16[32,32,256]{2,1,0:T(8,128)(2,1)} %get-tuple-element.28) | copy-start | bytes 1572868
  61.0 4.2 %collective-permute-start.5 = (f32[640,512]{1,0:T(8,128)S(1)}, f32[640,512]{1,0:T(8,128)S(1)}, u32[]{:S(2)}, u32[]{:S(2)}) collective-permute-start(f32[640,512]{1,0:T(8,128)S(1)} %slice_select_fusion), channel_id=1, source_target_pairs={{0,1},{1,0},{2,3},{3,2},{4,5},{5,4},{6,7},{7,6},{8,9},{9,8},{10,11... | collective-permute-start | bytes 3932168 | tf_op jit(solution)/shard_map/ppermute | solution.py:14
  65.7 16.0 %collective-permute-start.6 = (f16[640,512]{1,0:T(8,128)(2,1)S(1)}, f16[640,512]{1,0:T(8,128)(2,1)S(1)}, u32[]{:S(2)}, u32[]{:S(2)}) collective-permute-start(f16[640,512]{1,0:T(8,128)(2,1)S(1)} %get-tuple-element.5), channel_id=1, source_target_pairs={{0,2},{1,3},{2,0},{3,1},{4,6},{5,7},{6,4},{7,5},{8,10},{9,11},{10,... | collective-permute-start | bytes 1966088 | tf_op jit(solution)/shard_map/ppermute | solution.py:14
  66.0 19.3 %copy-start.7 = (bf16[32,32,256]{2,1,0:T(8,128)(2,1)S(1)}, bf16[32,32,256]{2,1,0:T(8,128)(2,1)}, u32[]{:S(2)}) copy-start(bf16[32,32,256]{2,1,0:T(8,128)(2,1)} %get-tuple-element.29) | copy-start | bytes 1572868
  81.9 3.0 %collective-permute-start.7 = (bf16[80,8,512]{2,1,0:T(8,128)(2,1)S(1)}, bf16[80,8,512]{2,1,0:T(8,128)(2,1)S(1)}, u32[]{:S(2)}, u32[]{:S(2)}) collective-permute-start(bf16[80,8,512]{2,1,0:T(8,128)(2,1)S(1)} %fusion.10), channel_id=1, source_target_pairs={{0,1},{1,0},{2,3},{3,2},{4,5},{5,4},{6,7},{7,6},{8,9},{9,8},{10,11... | collective-permute-start | bytes 1966088 | tf_op jit(solution)/shard_map/ppermute | solution.py:14
  84.9 2.2 %slice-start.2 = ((s8[5242880]{0:T(1024)(128)(4,1)}), s8[4194304]{0:T(1024)(128)(4,1)S(1)}, s32[]{:S(2)}) async-start(s8[5242880]{0:T(1024)(128)(4,1)} %bitcast.39), calls=%async_computation.2 | async-start | bytes 8388608
  85.3 2.2 %slice-start.3 = ((s8[5242880]{0:T(1024)(128)(4,1)}), s8[1048576]{0:T(1024)(128)(4,1)S(1)}, s32[]{:S(2)}) async-start(s8[5242880]{0:T(1024)(128)(4,1)} %bitcast.39), calls=%async_computation.3 | async-start | bytes 2097152

commit v2 on v1

--- a/solution.py
+++ b/solution.py
@@ -3,6 +3,8 @@
 import jax
 import jax.numpy as jnp
 from jax import lax
+from jax.experimental import pallas as pl
+from jax.experimental.pallas import tpu as pltpu
 from jax.sharding import PartitionSpec as P
 
 KC = 256
@@ -46,6 +48,71 @@
     return jnp.where(waves[None, :] <= cutoffs[:, None], weights[None, :], jnp.float32(0.0))
 
 
+def step_kernel(
+    state, weights, north, south, west, east, table, stepped, partial, rounded
+):
+    fields, levels, rows, columns = state.shape
+    lane = lax.broadcasted_iota(jnp.int32, (rows, columns), 1)
+    line = lax.broadcasted_iota(jnp.int32, (rows, columns), 0)
+
+    def one_field(field, carry):
+        above = north[field].astype(jnp.float32)
+        below = south[field].astype(jnp.float32)
+        left = west[0, field]
+        right = east[0, field]
+        for level in range(0, levels, 2):
+            pair = []
+            for at in (level, level + 1):
+                x = state[field, at]
+                w = jnp.where(lane == 0, left[:, at : at + 1], pltpu.roll(x, 1, 1))
+                e = jnp.where(
+                    lane == columns - 1, right[:, at : at + 1], pltpu.roll(x, columns - 1, 1)
+                )
+                n = jnp.where(line == 0, above[at : at + 1], pltpu.roll(x, 1, 0))
+                s = jnp.where(line == rows - 1, below[at : at + 1], pltpu.roll(x, rows - 1, 0))
+                y = (
+                    x
+                    + weights[0, at] * (e - x)
+                    + weights[1, at] * (w - x)
+                    + weights[2, at] * (n - x)
+                    + weights[3, at] * (s - x)
+                )
+                stepped[field, at] = y
+                pair.append(y)
+            first = pl.multiple_of(field * (levels * rows) + level * rows, 2 * rows)
+            rounded[pl.ds(first, 2 * rows), :] = jnp.concatenate(pair, axis=0).astype(
+                jnp.bfloat16
+            )
+        return carry
+
+    lax.fori_loop(0, fields, one_field, 0)
+    partial[0] = jnp.dot(rounded[...], table[...], preferred_element_type=jnp.float32)
+
+
+def merge_kernel(keep, spectra, table, stepped, merged):
+    fields, levels, rows, columns = stepped.shape
+    for field in range(fields):
+        first = field * levels * rows
+        smooth = lax.dot_general(
+            spectra[0, first : first + levels * rows],
+            table[...],
+            (((1,), (1,)), ((), ())),
+            preferred_element_type=jnp.float32,
+        )
+        smooth = smooth.astype(jnp.bfloat16).astype(jnp.float32)
+        smooth = smooth.reshape(levels, rows, columns)
+        kept = jnp.broadcast_to(keep[...], (rows, columns))[None] != 0
+        merged[field] = jnp.where(kept, smooth, stepped[field])
+
+
+def chunk_of(fields, levels, rows, columns, size):
+    return pl.BlockSpec((fields, size, rows, columns), lambda i: (0, i, 0, 0))
+
+
+def whole(*shape):
+    return pl.BlockSpec(shape, lambda i: (0,) * len(shape), pipeline_mode=pl.Buffered(1))
+
+
 def on_device(state_fields, stencil_weights, filter_mask, cutoff_wave):
     fields, levels, rows, columns = state_fields.shape
     lat_count, lon_count = lax.axis_size("lat"), lax.axis_size("lon")
@@ -54,33 +121,52 @@
     bits = lon_count.bit_length() - 1
     first_row = state_fields[:, :, 0]
     last_row = state_fields[:, :, -1]
-    signs = jnp.where(jnp.arange(fields) < 2, -1.0, 1.0).astype(jnp.float32)[:, None, None]
+    signs = jnp.where(jnp.arange(fields) < 2, -1.0, 1.0).astype(jnp.bfloat16)[:, None, None]
     pole_row = jnp.where(lat_pos == 0, first_row, last_row).astype(jnp.bfloat16)
-    over_pole = signs * flip(pole_row, "lon", bits - 1).astype(jnp.float32)
-    north_in = shift(last_row.astype(jnp.bfloat16), "lat", 1, False).astype(jnp.float32)
-    south_in = shift(first_row.astype(jnp.bfloat16), "lat", -1, False).astype(jnp.float32)
+    over_pole = flip(signs * pole_row, "lon", bits - 1)
+    north_in = shift(last_row.astype(jnp.bfloat16), "lat", 1, False)
+    south_in = shift(first_row.astype(jnp.bfloat16), "lat", -1, False)
     north_edge = jnp.where(lat_pos == 0, over_pole, north_in)
     south_edge = jnp.where(lat_pos == lat_count - 1, over_pole, south_in)
-    west_in = shift(state_fields[..., -1], "lon", 1, True)
-    east_in = shift(state_fields[..., 0], "lon", -1, True)
-    north_side = jnp.concatenate([north_edge[:, :, None], state_fields[:, :, :-1]], axis=2)
-    south_side = jnp.concatenate([state_fields[:, :, 1:], south_edge[:, :, None]], axis=2)
-    west_side = jnp.concatenate([west_in[..., None], state_fields[..., :-1]], axis=3)
-    east_side = jnp.concatenate([state_fields[..., 1:], east_in[..., None]], axis=3)
-    stepped = (
-        state_fields
-        + stencil_weights[0] * (east_side - state_fields)
-        + stencil_weights[1] * (west_side - state_fields)
-        + stencil_weights[2] * (north_side - state_fields)
-        + stencil_weights[3] * (south_side - state_fields)
-    )
+    size = 8
+    steps = levels // size
+
+    def columns_of(edge):
+        return edge.reshape(fields, steps, size, rows).transpose(1, 0, 3, 2)
+
+    west_in = shift(columns_of(state_fields[..., -1]), "lon", 1, True)
+    east_in = shift(columns_of(state_fields[..., 0]), "lon", -1, True)
     items = fields * levels
     start = lat_pos * rows
     cuts = lax.dynamic_slice_in_dim(cutoff_wave, start, rows)
     mask = lax.dynamic_slice_in_dim(filter_mask, start, rows)
     table = wave_table(lon_pos * columns, columns, circle_size)
-    rounded = stepped.astype(jnp.bfloat16).reshape(items * rows, columns)
-    partial = jnp.dot(rounded, table, preferred_element_type=jnp.float32)
+    rows_each = fields * size * rows
+    halo = pl.BlockSpec((fields, size, columns), lambda i: (0, i, 0))
+    side = pl.BlockSpec((1, fields, rows, size), lambda i: (i, 0, 0, 0))
+    stepped, partial = pl.pallas_call(
+        step_kernel,
+        grid=(steps,),
+        in_specs=[
+            chunk_of(fields, levels, rows, columns, size),
+            chunk_of(4, levels, rows, columns, size),
+            halo,
+            halo,
+            side,
+            side,
+            whole(columns, 2 * KC),
+        ],
+        out_specs=[
+            chunk_of(fields, levels, rows, columns, size),
+            pl.BlockSpec((1, rows_each, 2 * KC), lambda i: (i, 0, 0)),
+        ],
+        out_shape=[
+            jax.ShapeDtypeStruct(state_fields.shape, jnp.float32),
+            jax.ShapeDtypeStruct((steps, rows_each, 2 * KC), jnp.float32),
+        ],
+        scratch_shapes=[pltpu.VMEM((rows_each, columns), jnp.bfloat16)],
+        name="step",
+    )(state_fields, stencil_weights, north_edge, south_edge, west_in, east_in, table)
     halves = partial.reshape(2, items * rows // 2, 2 * KC)
     low = lon_pos % 2 == 0
     mine = jnp.where(low, halves[0], halves[1])
@@ -92,12 +178,20 @@
     other = flip(spectra, "lon", 0)
     spectra = jnp.concatenate(
         [jnp.where(low, spectra, other), jnp.where(low, other, spectra)], axis=0
-    ).reshape(-1, 2 * KC)
-    smooth = lax.dot_general(
-        spectra, table, (((1,), (1,)), ((), ())), preferred_element_type=jnp.float32
-    )
-    smooth = smooth.astype(jnp.bfloat16).reshape(fields, levels, rows, columns)
-    return jnp.where(mask[None, None, :, None] == 1, smooth.astype(jnp.float32), stepped)
+    ).reshape(steps, rows_each, 2 * KC)
+    return pl.pallas_call(
+        merge_kernel,
+        grid=(steps,),
+        in_specs=[
+            whole(rows, 1),
+            pl.BlockSpec((1, rows_each, 2 * KC), lambda i: (i, 0, 0)),
+            whole(columns, 2 * KC),
+            chunk_of(fields, levels, rows, columns, size),
+        ],
+        out_specs=chunk_of(fields, levels, rows, columns, size),
+        out_shape=jax.ShapeDtypeStruct(state_fields.shape, jnp.float32),
+        name="merge",
+    )(mask[:, None], spectra, table, stepped)
 
 
 def solution(mesh):

time: 91.1 us -> 82.3 us (0.903); the launches traced: 90.8 us -> 80.7 us
  local copies, waits for them, and re-layouts: 32.6 us -> 9.26 us
  Pallas kernels: 0 us -> 21.2 us
  other arithmetic: 22.8 us -> 10.1 us
  waiting for transfers between devices: 19.8 us -> 30.4 us
  matrix products: 3.1 us -> 0 us
  starting transfers between devices: 12.2 us -> 9.59 us
    pallas_call x0 -> x2, Pallas kernels: none -> 21.2 us  [the longest x1 11.3 us: on_device(): pl.pallas_call(step_kernel, grid=(steps,), in_specs=[chunk_of(fields, lev...]
    slice x4 -> x2, local copies, waits for them, and re-layouts: 23.4 us -> 7.41 us  [the longest x1 5.51 us: on_device(): first_row = state_fields[:, :, 0]]
    convert_element_type x2 -> x1, other arithmetic: 14.8 us -> 0.01 us  [on_device(): jnp.where(jnp.arange(fields) < 2, -1.0, 1.0).astype(jnp.bfloat16)]
    ppermute x4, waiting for transfers between devices: 0.01 us -> 10.7 us  [shift(): return lax.ppermute(block, axis, route)]
    broadcast_in_dim x4 -> x2, local copies, waits for them, and re-layouts: 5.15 us -> 0.75 us  [on_device(): mask[:, None]]
    dot_general x2 -> x0, matrix products: 3.1 us -> none  [the longest x1 1.56 us: on_device(): lax.dot_general(spectra, table, (((1,), (1,)), ((), ())), preferred_eleme...]
    concatenate x0 -> x2, other arithmetic: none -> 2.27 us  [the longest x1 1.22 us: on_device(): jnp.concatenate([jnp.where(low, spectra, other), jnp.where(low, other, sp...]
    ppermute x4, starting transfers between devices: 4.42 us -> 2.43 us  [flip(): return lax.ppermute(block, axis, route)]
  transfers between devices with their start and end apart: 8 -> 8, of which waited for: 3 -> 5; matrix products, arithmetic and copies ran while one was open for 30% -> 12% of each run, Pallas kernels for 0% -> 0%
where the time goes in v2:
time: 82.3 us; the launch traced here: 80.7 us
  waiting for transfers between devices  30.4 us (37%)
  Pallas kernels  21.2 us (26%)
  other arithmetic  10.1 us (12%)
  starting transfers between devices  9.59 us (12%)
  local copies, waits for them, and re-layouts  9.26 us (11%)
    ppermute x4, waiting for transfers between devices, flip(): return lax.ppermute(block, axis, route)  19.7 us
    pallas_call x1, Pallas kernels, on_device(): pl.pallas_call(step_kernel, grid=(steps,), in_specs=[chunk_of(fields, lev...  11.3 us
    ppermute x4, waiting for transfers between devices, shift(): return lax.ppermute(block, axis, route)  10.7 us
    pallas_call x1, Pallas kernels, on_device(): pl.pallas_call(merge_kernel, grid=(steps,), in_specs=[whole(rows, 1), pl....  9.83 us
    ppermute x4, starting transfers between devices, shift(): return lax.ppermute(block, axis, route)  7.16 us
    slice x1, local copies, waits for them, and re-layouts, on_device(): first_row = state_fields[:, :, 0]  5.51 us
    ppermute x4, starting transfers between devices, flip(): return lax.ppermute(block, axis, route)  2.43 us
    select_n x1, other arithmetic, on_device(): mine = jnp.where(low, halves[0], halves[1])  2 us
  transfers between devices with their start and end apart: 8, of which 5 were waited for; matrix products, arithmetic and copies ran while one was open for 12% of the time, Pallas kernels for 0%

profile of v2, /device:TPU:9, one launch (start us, length us, event | category | flops | bytes accessed | tf_op | source)
XLA Modules:
  0.0 80.7 jit_solution(6884272122863829426)
XLA Ops:
  0.0 0.0 copy-start
  0.0 1.9 %slice_reduce_fusion = (f32[5,32,8]{2,1,0:T(8,128)S(1)}, f32[5,32,8]{2,1,0:T(8,128)S(1)}) fusion(f32[5,32,8,1024]{3,2,1,0:T(8,128)} %state.1), kind=kLoop, calls=%fused_computation.9 | loop fusion | bytes 20480 | tf_op jit(solution)/shard_map/slice | solution.py:138
  1.9 0.1 copy.11
  2.0 1.8 %collective-permute-start.3 = (f32[4,5,8,8]{3,2,1,0:T(8,128)S(1)}, f32[4,5,8,8]{3,2,1,0:T(8,128)S(1)}, u32[]{:S(2)}, u32[]{:S(2)}) collective-permute-start(f32[4,5,8,8]{3,2,1,0:T(8,128)S(1)} %bitcast.42), channel_id=1, source_target_pairs={{0,1},{1,2},{2,3},{3,0},{4,5},{5,6},{6,7},{7,4},{8,9},{9,10},{10,1... | collective-permute-start | bytes 15368 | tf_op jit(solution)/shard_map/ppermute | solution.py:22
  3.8 0.1 copy.13
  3.9 0.1 collective-permute-start.4
  4.0 5.5 %fusion.26 = (bf16[5,32,1,1024]{3,2,1,0:T(2,128)(2,1)S(1)}, bf16[5,32,1,1024]{3,2,1,0:T(2,128)(2,1)S(1)}) fusion(f32[5,32,8,1024]{3,2,1,0:T(8,128)} %state.1), kind=kLoop, calls=%fused_computation.56 | loop fusion | bytes 1310720 | tf_op jit(solution)/shard_map/slice | solution.py:122
  9.5 0.1 copy.37
  9.6 3.0 %collective-permute-start.2 = (bf16[5,32,1024]{2,1,0:T(8,128)(2,1)S(1)}, bf16[5,32,1024]{2,1,0:T(8,128)(2,1)S(1)}, u32[]{:S(2)}, u32[]{:S(2)}) collective-permute-start(bf16[5,32,1024]{2,1,0:T(8,128)(2,1)S(1)} %bitcast.40), channel_id=1, source_target_pairs={{4,0},{8,4},{12,8},{16,12},{20,16},{24,20},{28,24},{5,1},{9,5},{13... | collective-permute-start | bytes 983048 | tf_op jit(solution)/shard_map/ppermute | solution.py:22
  12.6 0.1 copy.38
  12.8 2.2 %collective-permute-start.1 = (bf16[5,32,1024]{2,1,0:T(8,128)(2,1)S(1)}, bf16[5,32,1024]{2,1,0:T(8,128)(2,1)S(1)}, u32[]{:S(2)}, u32[]{:S(2)}) collective-permute-start(bf16[5,32,1024]{2,1,0:T(8,128)(2,1)S(1)} %bitcast.41), channel_id=1, source_target_pairs={{0,4},{4,8},{8,12},{12,16},{16,20},{20,24},{24,28},{1,5},{5,9},{9,... | collective-permute-start | bytes 983048 | tf_op jit(solution)/shard_map/ppermute | solution.py:22
  15.0 0.2 fusion.5
  15.2 0.3 collective-permute-start
  15.6 0.1 fusion.18
  15.7 0.2 fusion.21
  16.0 0.4 subtract_convert_fusion
  16.3 1.0 %pad_maximum_fusion.1.table = bf16[1024,512]{1,0:T(8,128)(2,1)} fusion(bf16[1024,256]{1,0:T(8,128)(2,1)S(1)} %bitcast.36, bf16[1024,256]{1,0:T(8,128)(2,1)S(1)} %bitcast.35), kind=kLoop, calls=%fused_computation.6 | loop fusion | flops 2097152 | bytes 2097152 | tf_op jit(solution)/shard_map/concatenate | solution.py:39
  17.4 9.8 %collective-permute-done.2 = bf16[5,32,1024]{2,1,0:T(8,128)(2,1)S(1)} collective-permute-done((bf16[5,32,1024]{2,1,0:T(8,128)(2,1)S(1)}, bf16[5,32,1024]{2,1,0:T(8,128)(2,1)S(1)}, u32[]{:S(2)}, u32[]{:S(2)}) %collective-permute-start.2) | collective-permute-done | bytes 327712 | tf_op jit(solution)/shard_map/ppermute | solution.py:22
  27.2 0.9 %collective-permute-done.1 = bf16[5,32,1024]{2,1,0:T(8,128)(2,1)S(1)} collective-permute-done((bf16[5,32,1024]{2,1,0:T(8,128)(2,1)S(1)}, bf16[5,32,1024]{2,1,0:T(8,128)(2,1)S(1)}, u32[]{:S(2)}, u32[]{:S(2)}) %collective-permute-start.1) | collective-permute-done | bytes 327712 | tf_op jit(solution)/shard_map/ppermute | solution.py:22
  28.1 0.0 collective-permute-done
  28.1 0.9 %broadcast_select_fusion.2 = (bf16[5,32,1024]{2,1,0:T(8,128)(2,1)}, bf16[5,32,1024]{2,1,0:T(8,128)(2,1)}) fusion(bf16[5,32,1024]{2,1,0:T(8,128)(2,1)S(1)} %collective-permute-done, bf16[5,32,1024]{2,1,0:T(8,128)(2,1)S(1)} %collective-permute-done.2, pred[]{:T(512)S(6)} %eq.27, bf16[5,32,1024]{2,1,0:T(8,128)(2,1)S(1)} %collective-permute-done.1, pred[]{:T(512)S(6)} %eq.26), kind=kLoop, calls=%fused_computation.21 | loop fusion | flops 327680 | bytes 1638402 | tf_op jit(solution)/shard_map/jit(_where)/select_n | solution.py:130
  29.0 0.0 collective-permute-done.3.west
  29.0 0.0 copy-start.1
  29.0 0.0 collective-permute-done.4.east
  29.0 0.0 copy-start.2
  29.0 0.6 copy-done.1
  29.7 0.0 copy-done.2
  29.7 11.3 %step.1 = (f32[5,32,8,1024]{3,2,1,0:T(8,128)}, f32[4,320,512]{2,1,0:T(8,128)}) custom-call(f32[5,32,8,1024]{3,2,1,0:T(8,128)} %state.1, f32[4,32,8,1024]{3,2,1,0:T(8,128)} %weights.1, bf16[5,32,1024]{2,1,0:T(8,128)(2,1)} %get-tuple-element.18.north, bf16[5,32,1024]{2,1,0:T(8,128)(2,1)} %get-tuple-element.17.south, f32[4,5,8,8]{3,2,1,0:T(8,128)} %copy-done.1, ...), custom_call_target="tpu_custom_call" | custom-call | tf_op jit(solution)/shard_map/step/pallas_call | solution.py:147
  41.0 2.0 %slice_select_fusion.1 = (f32[2,320,512]{2,1,0:T(8,128)S(1)}, f32[2,320,512]{2,1,0:T(8,128)S(1)}) fusion(f32[4,320,512]{2,1,0:T(8,128)} %get-tuple-element.7, pred[]{:T(512)S(6)} %eq.25), kind=kLoop, calls=%fused_computation.5 | loop fusion | flops 655360 | bytes 5242881 | tf_op jit(solution)/shard_map/jit(_where)/select_n | solution.py:172
  43.0 0.6 collective-permute-start.5
  43.6 2.7 %collective-permute-done.5 = f32[640,512]{1,0:T(8,128)S(1)} collective-permute-done((f32[640,512]{1,0:T(8,128)S(1)}, f32[640,512]{1,0:T(8,128)S(1)}, u32[]{:S(2)}, u32[]{:S(2)}) %collective-permute-start.5) | collective-permute-done | bytes 1310752 | tf_op jit(solution)/shard_map/ppermute | solution.py:16
  46.3 0.0 copy-start.3
  46.3 1.2 %fusion.1 = f16[640,512]{1,0:T(8,128)(2,1)} fusion(f32[640,512]{1,0:T(8,128)S(1)} %collective-permute-done.5, f32[2,320,512]{2,1,0:T(8,128)S(1)} %get-tuple-element.13), kind=kLoop, calls=%fused_computation.16 | loop fusion | flops 655360 | bytes 3276800 | tf_op jit(solution)/shard_map/convert_element_type | solution.py:175
  47.5 0.3 collective-permute-start.6
  47.7 0.0 copy-done.3
  47.7 0.1 dynamic_slice.7
  47.8 0.1 compare_select_fusion
  47.9 15.7 %collective-permute-done.6 = f16[640,512]{1,0:T(8,128)(2,1)S(1)} collective-permute-done((f16[640,512]{1,0:T(8,128)(2,1)}, f16[640,512]{1,0:T(8,128)(2,1)S(1)}, u32[]{:S(2)}, u32[]{:S(2)}) %collective-permute-start.6) | collective-permute-done | bytes 655392 | tf_op jit(solution)/shard_map/ppermute | solution.py:16
  63.6 1.2 %fusion = bf16[80,8,512]{2,1,0:T(8,128)(2,1)} fusion(f16[640,512]{1,0:T(8,128)(2,1)S(1)} %collective-permute-done.6, f32[8,512]{1,0:T(8,128)S(1)} %compare_select_fusion, f32[640,512]{1,0:T(8,128)S(1)} %collective-permute-done.5, f32[2,320,512]{2,1,0:T(8,128)S(1)} %get-tuple-element.13), kind=kLoop, calls=%fused_computation.2 | loop fusion | flops 1638400 | bytes 3948544 | tf_op jit(solution)/shard_map/convert_element_type | solution.py:177
  64.8 1.2 %collective-permute-start.7 = (bf16[80,8,512]{2,1,0:T(8,128)(2,1)}, bf16[80,8,512]{2,1,0:T(8,128)(2,1)}, u32[]{:S(2)}, u32[]{:S(2)}) collective-permute-start(bf16[80,8,512]{2,1,0:T(8,128)(2,1)} %fusion), channel_id=1, source_target_pairs={{0,1},{1,0},{2,3},{3,2},{4,5},{5,4},{6,7},{7,6},{8,9},{9,8},{10,11... | collective-permute-start | bytes 1966088 | tf_op jit(solution)/shard_map/ppermute | solution.py:16
  66.1 0.0 copy-done
  66.1 0.1 dynamic-slice_bitcast_fusion
  66.1 0.7 copy.14.keep
  66.8 1.3 %collective-permute-done.7 = bf16[80,8,512]{2,1,0:T(8,128)(2,1)} collective-permute-done((bf16[80,8,512]{2,1,0:T(8,128)(2,1)}, bf16[80,8,512]{2,1,0:T(8,128)(2,1)}, u32[]{:S(2)}, u32[]{:S(2)}) %collective-permute-start.7) | collective-permute-done | bytes 655392 | tf_op jit(solution)/shard_map/ppermute | solution.py:16
  68.1 1.6 %broadcast_select_fusion.1 = (bf16[80,8,512]{2,1,0:T(8,128)(2,1)S(1)}, bf16[80,8,512]{2,1,0:T(8,128)(2,1)S(1)}) fusion(bf16[80,8,512]{2,1,0:T(8,128)(2,1)} %collective-permute-done.7, pred[]{:T(512)S(6)} %eq.25, f32[8,512]{1,0:T(8,128)S(1)} %compare_select_fusion, f16[640,512]{1,0:T(8,128)(2,1)S(1)} %collective-permute-done.6, ...), kind=kLoop, calls=%fused_computation.13 | loop fusion | flops 2293760 | bytes 5259265 | tf_op jit(solution)/shard_map/jit(_where)/select_n | solution.py:180
  69.7 1.2 %pad_maximum_fusion = bf16[160,8,512]{2,1,0:T(8,128)(2,1)} fusion(bf16[80,8,512]{2,1,0:T(8,128)(2,1)S(1)} %get-tuple-element.16, bf16[80,8,512]{2,1,0:T(8,128)(2,1)S(1)} %get-tuple-element.15), kind=kLoop, calls=%fused_computation | loop fusion | flops 655360 | bytes 2621440 | tf_op jit(solution)/shard_map/concatenate | solution.py:179
  70.9 9.8 %merge.1 = f32[5,32,8,1024]{3,2,1,0:T(8,128)} custom-call(s32[8,1]{1,0:T(8,128)} %copy.14.keep, bf16[4,320,512]{2,1,0:T(8,128)(2,1)} %bitcast.34, bf16[1024,512]{1,0:T(8,128)(2,1)} %pad_maximum_fusion.1.table, f32[5,32,8,1024]{3,2,1,0:T(8,128)} %get-tuple-element.8.stepped), custom_call_target="tpu_custom_call" | custom-call | tf_op jit(solution)/shard_map/merge/pallas_call | solution.py:182
  (4 shorter events, 0.0 us)
Async XLA Ops:
  0.0 66.1 %copy-start = (s32[64]{0:T(128)S(1)}, s32[64]{0:T(128)}, u32[]{:S(2)}) copy-start(s32[64]{0:T(128)} %param.6) | copy-start | bytes 772
  2.0 27.0 %collective-permute-start.3 = (f32[4,5,8,8]{3,2,1,0:T(8,128)S(1)}, f32[4,5,8,8]{3,2,1,0:T(8,128)S(1)}, u32[]{:S(2)}, u32[]{:S(2)}) collective-permute-start(f32[4,5,8,8]{3,2,1,0:T(8,128)S(1)} %bitcast.42), channel_id=1, source_target_pairs={{0,1},{1,2},{2,3},{3,0},{4,5},{5,6},{6,7},{7,4},{8,9},{9,10},{10,1... | collective-permute-start | bytes 15368 | tf_op jit(solution)/shard_map/ppermute | solution.py:22
  3.9 25.1 %collective-permute-start.4 = (f32[4,5,8,8]{3,2,1,0:T(8,128)S(1)}, f32[4,5,8,8]{3,2,1,0:T(8,128)S(1)}, u32[]{:S(2)}, u32[]{:S(2)}) collective-permute-start(f32[4,5,8,8]{3,2,1,0:T(8,128)S(1)} %bitcast.43), channel_id=1, source_target_pairs={{0,3},{1,0},{2,1},{3,2},{4,7},{5,4},{6,5},{7,6},{8,11},{9,8},{10,9... | collective-permute-start | bytes 15368 | tf_op jit(solution)/shard_map/ppermute | solution.py:22
  9.6 17.5 %collective-permute-start.2 = (bf16[5,32,1024]{2,1,0:T(8,128)(2,1)S(1)}, bf16[5,32,1024]{2,1,0:T(8,128)(2,1)S(1)}, u32[]{:S(2)}, u32[]{:S(2)}) collective-permute-start(bf16[5,32,1024]{2,1,0:T(8,128)(2,1)S(1)} %bitcast.40), channel_id=1, source_target_pairs={{4,0},{8,4},{12,8},{16,12},{20,16},{24,20},{28,24},{5,1},{9,5},{13... | collective-permute-start | bytes 983048 | tf_op jit(solution)/shard_map/ppermute | solution.py:22
  12.8 15.3 %collective-permute-start.1 = (bf16[5,32,1024]{2,1,0:T(8,128)(2,1)S(1)}, bf16[5,32,1024]{2,1,0:T(8,128)(2,1)S(1)}, u32[]{:S(2)}, u32[]{:S(2)}) collective-permute-start(bf16[5,32,1024]{2,1,0:T(8,128)(2,1)S(1)} %bitcast.41), channel_id=1, source_target_pairs={{0,4},{4,8},{8,12},{12,16},{16,20},{20,24},{24,28},{1,5},{5,9},{9,... | collective-permute-start | bytes 983048 | tf_op jit(solution)/shard_map/ppermute | solution.py:22
  15.2 12.9 %collective-permute-start = (bf16[5,32,1024]{2,1,0:T(8,128)(2,1)S(1)}, bf16[5,32,1024]{2,1,0:T(8,128)(2,1)S(1)}, u32[]{:S(2)}, u32[]{:S(2)}) collective-permute-start(bf16[5,32,1024]{2,1,0:T(8,128)(2,1)S(1)} %fusion.5), channel_id=1, source_target_pairs={{0,2},{1,3},{2,0},{3,1},{4,6},{5,7},{6,4},{7,5},{8,10},{9,11},{10,... | collective-permute-start | bytes 983048 | tf_op jit(solution)/shard_map/ppermute | solution.py:16
  29.0 0.6 copy-start.1
  29.0 0.6 copy-start.2
  43.0 3.3 %collective-permute-start.5 = (f32[640,512]{1,0:T(8,128)S(1)}, f32[640,512]{1,0:T(8,128)S(1)}, u32[]{:S(2)}, u32[]{:S(2)}) collective-permute-start(f32[640,512]{1,0:T(8,128)S(1)} %bitcast.37), channel_id=1, source_target_pairs={{0,1},{1,0},{2,3},{3,2},{4,5},{5,4},{6,7},{7,6},{8,9},{9,8},{10,11... | collective-permute-start | bytes 3932168 | tf_op jit(solution)/shard_map/ppermute | solution.py:16
  46.3 1.4 %copy-start.3 = (s32[64]{0:T(128)S(1)}, s32[64]{0:T(128)}, u32[]{:S(2)}) copy-start(s32[64]{0:T(128)} %param.7) | copy-start | bytes 772
  47.5 16.1 %collective-permute-start.6 = (f16[640,512]{1,0:T(8,128)(2,1)}, f16[640,512]{1,0:T(8,128)(2,1)S(1)}, u32[]{:S(2)}, u32[]{:S(2)}) collective-permute-start(f16[640,512]{1,0:T(8,128)(2,1)} %fusion.1), channel_id=1, source_target_pairs={{0,2},{1,3},{2,0},{3,1},{4,6},{5,7},{6,4},{7,5},{8,10},{9,11},{10,... | collective-permute-start | bytes 1966088 | tf_op jit(solution)/shard_map/ppermute | solution.py:16
  64.8 3.3 %collective-permute-start.7 = (bf16[80,8,512]{2,1,0:T(8,128)(2,1)}, bf16[80,8,512]{2,1,0:T(8,128)(2,1)}, u32[]{:S(2)}, u32[]{:S(2)}) collective-permute-start(bf16[80,8,512]{2,1,0:T(8,128)(2,1)} %fusion), channel_id=1, source_target_pairs={{0,1},{1,0},{2,3},{3,2},{4,5},{5,4},{6,7},{7,6},{8,9},{9,8},{10,11... | collective-permute-start | bytes 1966088 | tf_op jit(solution)/shard_map/ppermute | solution.py:16

commit v3 on v1

v3 whole, which is shorter than its diff:
```python
import math

import jax
import jax.numpy as jnp
from jax import lax
from jax.experimental import pallas as pl
from jax.experimental.pallas import tpu as pltpu
from jax.sharding import PartitionSpec as P

KC = 256


def flip(block, axis, bit):
    count = lax.axis_size(axis)
    route = [(i, i ^ (1 << bit)) for i in range(count) if i ^ (1 << bit) < count]
    return lax.ppermute(block, axis, route)


def angle_parts(columns, circle_size):
    waves = jnp.arange(KC, dtype=jnp.int32)
    product = columns[:, None] * waves[None, :] % circle_size
    angles = product.astype(jnp.float32) * (2.0 * math.pi / circle_size)
    return jnp.cos(angles), jnp.sin(angles)


def wave_table(first, column_count, circle_size):
    fine = 32
    coarse = column_count // fine
    cos_c, sin_c = angle_parts(first + fine * jnp.arange(coarse, dtype=jnp.int32), circle_size)
    cos_f, sin_f = angle_parts(jnp.arange(fine, dtype=jnp.int32), circle_size)
    cos_c, sin_c = cos_c[:, None], sin_c[:, None]
    cos_f, sin_f = cos_f[None], sin_f[None]
    cosine = (cos_c * cos_f - sin_c * sin_f).astype(jnp.bfloat16).reshape(column_count, KC)
    sine = (sin_c * cos_f + cos_c * sin_f).astype(jnp.bfloat16).reshape(column_count, KC)
    return jnp.concatenate([cosine, sine], axis=1)


def mode_scale(cutoffs, circle_size):
    waves = jnp.arange(2 * KC, dtype=jnp.int32) % KC
    weights = jnp.where(waves == 0, 1.0 / circle_size, 2.0 / circle_size).astype(jnp.float32)
    return jnp.where(waves[None, :] <= cutoffs[:, None], weights[None, :], jnp.float32(0.0))


MESH = pl.DeviceIdType.MESH


def step_kernel(
    state,
    weights,
    table,
    stepped,
    totals,
    cells,
    planes,
    waves,
    results,
    rounded,
    top,
    bottom,
    north,
    south,
    columns_out,
    columns_in,
    sides,
    partial,
    arrived,
    load_sem,
    table_sem,
    row_send,
    row_recv,
    side_send,
    side_recv,
    sum_send,
    sum_recv,
    store_sem,
):
    chunks, fields, depth, columns = cells.shape
    size = top.shape[2]
    rows = depth // size
    half = partial.shape[1] // 2
    lat_count, lon_count = lax.axis_size("lat"), lax.axis_size("lon")
    lat, lon = lax.axis_index("lat"), lax.axis_index("lon")
    after = lax.rem(lon + 1, lon_count)
    before = lax.rem(lon + lon_count - 1, lon_count)
    across = lax.rem(lon + lon_count // 2, lon_count)
    odd = lax.rem(lon, 2)
    twin = lon + 1 - 2 * odd

    def load(g):
        part = pl.ds(pl.multiple_of(g * depth, depth), depth)
        return (
            pltpu.make_async_copy(state.at[:, part], cells.at[g], load_sem.at[0, g]),
            pltpu.make_async_copy(weights.at[:, part], planes.at[g], load_sem.at[1, g]),
        )

    def store(g):
        part = pl.ds(pl.multiple_of(g * depth, depth), depth)
        return pltpu.make_async_copy(results.at[g], stepped.at[:, part], store_sem.at[g])

    def remote(source, target, sent, got, device):
        return pltpu.make_async_remote_copy(
            src_ref=source,
            dst_ref=target,
            send_sem=sent,
            recv_sem=got,
            device_id=device,
            device_id_type=MESH,
        )

    def row_copy(g, up, device, into_north):
        return remote(
            top.at[g] if up else bottom.at[g],
            north.at[g] if into_north else south.at[g],
            row_send.at[0 if up else 1, g],
            row_recv.at[0 if into_north else 1, g],
            device,
        )

    def side_copy(k, device):
        return remote(
            columns_out.at[k], columns_in.at[k], side_send.at[k], side_recv.at[k], device
        )

    def sum_copy(g):
        away = pl.ds(pl.multiple_of((1 - odd) * half, 8), half)
        return remote(
            partial.at[g, away], arrived.at[g], sum_send.at[g], sum_recv.at[g], (lat, twin)
        )

    for g in range(chunks):
        load(g)[0].start()
    for g in range(chunks):
        load(g)[1].start()
    fetch_table = pltpu.make_async_copy(table, waves, table_sem)
    fetch_table.start()

    barrier = pltpu.get_barrier_semaphore()
    for other in (after, before, across, twin):
        pl.semaphore_signal(barrier, inc=1, device_id=(lat, other), device_id_type=MESH)

    @pl.when(lat > 0)
    def _():
        pl.semaphore_signal(barrier, inc=1, device_id=(lat - 1, lon), device_id_type=MESH)

    @pl.when(lat < lat_count - 1)
    def _():
        pl.semaphore_signal(barrier, inc=1, device_id=(lat + 1, lon), device_id_type=MESH)

    inside = (lat > 0) & (lat < lat_count - 1)

    @pl.when(inside)
    def _():
        pl.semaphore_wait(barrier, 6)

    @pl.when(jnp.logical_not(inside))
    def _():
        pl.semaphore_wait(barrier, 5)

    taker = lax.broadcasted_iota(jnp.int32, (2 * size, depth), 0)
    taken = lax.broadcasted_iota(jnp.int32, (2 * size, depth), 1)
    wanted = jnp.where(taker < size, taker * rows, (taker - size) * rows + rows - 1)
    gather = jnp.where(taken == wanted, 1.0, 0.0).astype(jnp.bfloat16)

    def send_rows(g, carry):
        load(g)[0].wait()
        for field in range(fields):
            sign = -1.0 if field < 2 else 1.0
            up_sign = jnp.where(lat == 0, sign, 1.0).astype(jnp.float32)
            down_sign = jnp.where(lat == lat_count - 1, sign, 1.0).astype(jnp.float32)
            edges = jnp.dot(
                gather,
                cells[g, field].astype(jnp.bfloat16),
                preferred_element_type=jnp.float32,
            )
            top[g, field] = (edges[:size] * up_sign).astype(jnp.bfloat16)
            bottom[g, field] = (edges[size:] * down_sign).astype(jnp.bfloat16)

        @pl.when(lat == 0)
        def _():
            row_copy(g, True, (lat, across), True).start()

        @pl.when(lat > 0)
        def _():
            row_copy(g, True, (lat - 1, lon), False).start()

        @pl.when(lat < lat_count - 1)
        def _():
            row_copy(g, False, (lat + 1, lon), True).start()

        @pl.when(lat == lat_count - 1)
        def _():
            row_copy(g, False, (lat, across), False).start()

        return carry

    lax.fori_loop(0, chunks, send_rows, 0)

    spot = lax.broadcasted_iota(jnp.int32, (16, 128), 1)
    line = lax.broadcasted_iota(jnp.int32, (16, 128), 0)

    def pick(k, lanes, lane):
        chosen = jnp.where((spot == lane) & (line == 0), 1.0, 0.0).astype(jnp.bfloat16)
        for g in range(chunks):
            for field in range(0, fields):
                first = (g * fields + field) * depth
                edge = cells[g, field, :, lanes].astype(jnp.bfloat16)
                picked = lax.dot_general(
                    chosen, edge, (((1,), (1,)), ((), ())), preferred_element_type=jnp.float32
                )
                columns_out[k, g * fields + field] = picked.astype(jnp.bfloat16)

    pick(0, pl.ds(columns - 128, 128), 127)
    side_copy(0, (lat, after)).start()
    pick(1, pl.ds(0, 128), 0)
    side_copy(1, (lat, before)).start()

    spread = jnp.where(line == 0, 1.0, 0.0).astype(jnp.bfloat16)
    for k in range(2):
        side_copy(k, (lat, after)).wait_recv()
        for at in range(chunks * fields):
            sides[k, at] = lax.dot_general(
                columns_in[k, at],
                spread,
                (((0,), (0,)), ((), ())),
                preferred_element_type=jnp.float32,
            )
    fetch_table.wait()

    lane = lax.broadcasted_iota(jnp.int32, (rows, columns), 1)
    level_line = lax.broadcasted_iota(jnp.int32, (rows, columns), 0)
    copies = columns // 128

    def one_chunk(g, carry):
        load(g)[1].wait()
        row_copy(g, True, (lat, across), True).wait_recv()
        row_copy(g, False, (lat, across), False).wait_recv()

        def one_field(field, inner):
            above = north[g, field].astype(jnp.float32)
            below = south[g, field].astype(jnp.float32)
            for level in range(0, size, 2):
                pair = []
                for at in (level, level + 1):
                    span = pl.ds(at * rows, rows)
                    x = cells[g, field, span]
                    left = jnp.concatenate([sides[0, g * fields + field, span]] * copies, axis=1)
                    right = jnp.concatenate([sides[1, g * fields + field, span]] * copies, axis=1)
                    w = jnp.where(lane == 0, left, pltpu.roll(x, 1, 1))
                    e = jnp.where(lane == columns - 1, right, pltpu.roll(x, columns - 1, 1))
                    n = jnp.where(level_line == 0, above[at : at + 1], pltpu.roll(x, 1, 0))
                    s = jnp.where(
                        level_line == rows - 1, below[at : at + 1], pltpu.roll(x, rows - 1, 0)
                    )
                    y = (
                        x
                        + planes[g, 0, span] * (e - x)
                        + planes[g, 1, span] * (w - x)
                        + planes[g, 2, span] * (n - x)
                        + planes[g, 3, span] * (s - x)
                    )
                    results[g, field, span] = y
                    pair.append(y)
                first = pl.multiple_of(field * depth + level * rows, 2 * rows)
                rounded[pl.ds(first, 2 * rows), :] = jnp.concatenate(pair, axis=0).astype(
                    jnp.bfloat16
                )
            return inner

        lax.fori_loop(0, fields, one_field, 0)
        store(g).start()
        partial[g] = jnp.dot(rounded[...], waves[...], preferred_element_type=jnp.float32)
        sum_copy(g).start()
        return carry

    lax.fori_loop(0, chunks, one_chunk, 0)

    def one_total(g, carry):
        sum_copy(g).wait_recv()
        mine = pl.ds(pl.multiple_of(odd * half, 8), half)
        totals[g] = partial[g, mine] + arrived[g]
        return carry

    lax.fori_loop(0, chunks, one_total, 0)

    def finish(g, carry):
        sum_copy(g).wait_send()
        row_copy(g, True, (lat, across), True).wait_send()
        row_copy(g, False, (lat, across), False).wait_send()
        store(g).wait()
        return carry

    lax.fori_loop(0, chunks, finish, 0)
    for k in range(2):
        side_copy(k, (lat, after)).wait_send()


def merge_kernel(keep, spectra, table, stepped, merged):
    fields, levels, rows, columns = stepped.shape
    smooth = jnp.dot(spectra[0], table[...], preferred_element_type=jnp.float32)
    smooth = smooth.astype(jnp.bfloat16).astype(jnp.float32)
    smooth = smooth.reshape(fields, levels, rows, columns)
    kept = jnp.broadcast_to(keep[...], (rows, columns)) != 0
    merged[...] = jnp.where(kept, smooth, stepped[...])


def chunk_of(fields, levels, rows, columns, size):
    return pl.BlockSpec((fields, size, rows, columns), lambda i: (0, i, 0, 0))


def whole(*shape):
    return pl.BlockSpec(shape, lambda i: (0,) * len(shape), pipeline_mode=pl.Buffered(1))


def on_device(state_fields, stencil_weights, filter_mask, cutoff_wave):
    fields, levels, rows, columns = state_fields.shape
    lat_count, lon_count = lax.axis_size("lat"), lax.axis_size("lon")
    lat_pos, lon_pos = lax.axis_index("lat"), lax.axis_index("lon")
    circle_size = columns * lon_count
    bits = lon_count.bit_length() - 1
    size = 8
    steps = levels // size
    start = lat_pos * rows
    cuts = lax.dynamic_slice_in_dim(cutoff_wave, start, rows)
    mask = lax.dynamic_slice_in_dim(filter_mask, start, rows)
    table = wave_table(lon_pos * columns, columns, circle_size)
    rows_each = fields * size * rows
    depth = size * rows
    anywhere = pl.BlockSpec(memory_space=pl.ANY)
    dma = pltpu.SemaphoreType.DMA
    strip = pltpu.VMEM((steps, fields, size, columns), jnp.bfloat16)
    column_strip = pltpu.VMEM((2, steps * fields, 16, depth), jnp.bfloat16)
    stepped, total = pl.pallas_call(
        step_kernel,
        in_specs=[anywhere] * 3,
        out_specs=[anywhere, pl.BlockSpec(memory_space=pltpu.VMEM)],
        out_shape=[
            jax.ShapeDtypeStruct((fields, levels * rows, columns), jnp.float32),
            jax.ShapeDtypeStruct((steps, rows_each // 2, 2 * KC), jnp.float32),
        ],
        scratch_shapes=[
            pltpu.VMEM((steps, fields, depth, columns), jnp.float32),
            pltpu.VMEM((steps, 4, depth, columns), jnp.float32),
            pltpu.VMEM((columns, 2 * KC), jnp.bfloat16),
            pltpu.VMEM((steps, fields, depth, columns), jnp.float32),
            pltpu.VMEM((rows_each, columns), jnp.bfloat16),
            strip,
            strip,
            strip,
            strip,
            column_strip,
            column_strip,
            pltpu.VMEM((2, steps * fields, depth, 128), jnp.float32),
            pltpu.VMEM((steps, rows_each, 2 * KC), jnp.float32),
            pltpu.VMEM((steps, rows_each // 2, 2 * KC), jnp.float32),
            dma((2, steps)),
            dma,
            dma((2, steps)),
            dma((2, steps)),
            dma((2,)),
            dma((2,)),
            dma((steps,)),
            dma((steps,)),
            dma((steps,)),
        ],
        compiler_params=pltpu.CompilerParams(collective_id=0, has_side_effects=True),
        name="step",
    )(
        state_fields.reshape(fields, levels * rows, columns),
        stencil_weights.reshape(4, levels * rows, columns),
        table,
    )
    stepped = stepped.reshape(state_fields.shape)
    low = lon_pos % 2 == 0
    for bit in range(1, bits):
        total = total + flip(total.astype(jnp.float16), "lon", bit).astype(jnp.float32)
    scale = mode_scale(cuts, circle_size)
    spectra = (total.reshape(steps, -1, rows, 2 * KC) * scale).astype(jnp.bfloat16)
    spectra = spectra.reshape(steps, -1, 2 * KC)
    other = flip(spectra, "lon", 0)
    spectra = jnp.concatenate(
        [jnp.where(low, spectra, other), jnp.where(low, other, spectra)], axis=1
    )
    back_table = table.T
    return pl.pallas_call(
        merge_kernel,
        grid=(steps,),
        in_specs=[
            whole(rows, 1),
            pl.BlockSpec((1, rows_each, 2 * KC), lambda i: (i, 0, 0)),
            whole(2 * KC, columns),
            chunk_of(fields, levels, rows, columns, size),
        ],
        out_specs=chunk_of(fields, levels, rows, columns, size),
        out_shape=jax.ShapeDtypeStruct(state_fields.shape, jnp.float32),
        name="merge",
    )(mask[:, None], spectra, back_table, stepped)


def solution(mesh):
    return jax.shard_map(
        on_device,
        mesh=mesh,
        in_specs=(P(None, None, "lat", "lon"), P(None, None, "lat", "lon"), P(), P()),
        out_specs=P(None, None, "lat", "lon"),
        check_vma=False,
    )
```

time: 91.1 us -> 55.7 us (0.61)
  local copies, waits for them, and re-layouts: 32.6 us -> 2.59 us
  Pallas kernels: 0 us -> 29.8 us
  other arithmetic: 22.8 us -> 4.98 us
  starting transfers between devices: 12.2 us -> 1.82 us
  waiting for transfers between devices: 19.8 us -> 16.2 us
  matrix products: 3.1 us -> 0 us
    pallas_call x0 -> x2, Pallas kernels: none -> 29.8 us  [the longest x1 23 us: on_device(): pl.pallas_call(step_kernel, in_specs=[anywhere] * 3, out_specs=[anywhere,...]
    slice x4 -> x0, local copies, waits for them, and re-layouts: 23.4 us -> none  [the longest x1 10.7 us: on_device(): state_fields[:, :, :-1]]
    convert_element_type x3 -> x2, other arithmetic: 15 us -> 0.62 us  [the longest x1 0.35 us: wave_table(): (cos_c * cos_f - sin_c * sin_f).astype(jnp.bfloat16)]
    ppermute x4 -> x0, starting transfers between devices: 7.82 us -> none  [shift(): return lax.ppermute(block, axis, route)]
    broadcast_in_dim x4 -> x2, local copies, waits for them, and re-layouts: 5.15 us -> 0.75 us  [on_device(): mask[:, None]]
    ppermute x4 -> x2, waiting for transfers between devices: 19.8 us -> 16.2 us  [flip(): return lax.ppermute(block, axis, route)]
    select_n x3 -> x0, other arithmetic: 3.57 us -> none  [the longest x1 3.29 us: on_device(): jnp.where(mask[None, None, :, None] == 1, smooth.astype(jnp.float32), ste...]
    dot_general x2 -> x0, matrix products: 3.1 us -> none  [the longest x1 1.56 us: on_device(): lax.dot_general(spectra, table, (((1,), (1,)), ((), ())), preferred_eleme...]
  transfers between devices with their start and end apart: 8 -> 2, of which waited for: 3 -> 2; matrix products, arithmetic and copies ran while one was open for 30% -> 2% of each run, Pallas kernels for 0% -> 0%
where the time goes in v3:
time: 55.7 us; the launch traced here: 55.5 us
  Pallas kernels  29.8 us (54%)
  waiting for transfers between devices  16.2 us (29%)
  other arithmetic  4.98 us (9%)
  local copies, waits for them, and re-layouts  2.59 us (5%)
  starting transfers between devices  1.82 us (3%)
    pallas_call x1, Pallas kernels, on_device(): pl.pallas_call(step_kernel, in_specs=[anywhere] * 3, out_specs=[anywhere,...  23 us
    ppermute x2, waiting for transfers between devices, flip(): return lax.ppermute(block, axis, route)  16.2 us
    pallas_call x1, Pallas kernels, on_device(): pl.pallas_call(merge_kernel, grid=(steps,), in_specs=[whole(rows, 1), pl....  6.73 us
    ppermute x2, starting transfers between devices, flip(): return lax.ppermute(block, axis, route)  1.82 us
    convert_element_type x1, other arithmetic, on_device(): total.astype(jnp.float16)  1.54 us
    concatenate x1, local copies, waits for them, and re-layouts, wave_table(): return jnp.concatenate([cosine, sine], axis=1)  1.32 us
    concatenate x1, other arithmetic, on_device(): jnp.concatenate([jnp.where(low, spectra, other), jnp.where(low, other, sp...  1.19 us
  transfers between devices with their start and end apart: 2, of which 2 were waited for; matrix products, arithmetic and copies ran while one was open for 2% of the time, Pallas kernels for 0%

profile of v3, /device:TPU:9, one launch (start us, length us, event | category | flops | bytes accessed | tf_op | source)
XLA Modules:
  0.0 55.5 jit_solution(6139599496527750302)
XLA Ops:
  0.0 0.0 copy-start
  0.0 0.1 fusion.12
  0.2 0.2 fusion.15
  0.4 0.3 subtract_convert_fusion
  0.7 0.2 copy.7
  0.9 0.2 copy.8
  1.2 1.1 %fusion.19 = (bf16[512,1024]{1,0:T(8,128)(2,1)}, bf16[1024,512]{0,1:T(8,128)(2,1)S(1)}) fusion(bf16[1024,256]{0,1:T(8,128)(2,1)S(1)} %copy.8, bf16[1024,256]{0,1:T(8,128)(2,1)S(1)} %copy.7), kind=kLoop, calls=%fused_computation.39 | loop fusion | flops 2097152 | bytes 3145728 | tf_op jit(solution)/shard_map/transpose | solution.py:383
  2.3 1.3 %copy.9.table = bf16[1024,512]{1,0:T(8,128)(2,1)} copy(bf16[1024,512]{0,1:T(8,128)(2,1)S(1)} %get-tuple-element.12) | data formatting | bytes 2097152 | tf_op jit(solution)/shard_map/concatenate | solution.py:35
  3.6 0.0 copy-start.2
  3.6 23.0 %step.1 = (f32[5,256,1024]{2,1,0:T(8,128)}, f32[4,160,512]{2,1,0:T(8,128)}) custom-call(f32[5,256,1024]{2,1,0:T(8,128)} %bitcast.11, f32[4,256,1024]{2,1,0:T(8,128)} %bitcast.13, bf16[1024,512]{1,0:T(8,128)(2,1)} %copy.9.table), custom_call_target="tpu_custom_call" | custom-call | tf_op jit(solution)/shard_map/step/pallas_call | solution.py:332
  26.6 0.0 copy-start.1
  26.6 1.5 %convert_element_type.56 = f16[4,160,512]{2,1,0:T(8,128)(2,1)S(1)} convert(f32[4,160,512]{2,1,0:T(8,128)} %get-tuple-element.7) | non-fusion elementwise | flops 327680 | bytes 1966080 | tf_op jit(solution)/shard_map/convert_element_type | solution.py:375
  28.2 0.8 %collective-permute-start = (f16[4,160,512]{2,1,0:T(8,128)(2,1)S(1)}, f16[4,160,512]{2,1,0:T(8,128)(2,1)S(1)}, u32[]{:S(2)}, u32[]{:S(2)}) collective-permute-start(f16[4,160,512]{2,1,0:T(8,128)(2,1)S(1)} %convert_element_type.56), channel_id=1, source_target_pairs={{0,2},{1,3},{2,0},{3,1},{4,6},{5,7},{6,4},{7,5},{8,10},{9,11},{10,... | collective-permute-start | bytes 1966088 | tf_op jit(solution)/shard_map/ppermute | solution.py:16
  29.0 0.0 copy-done.2
  29.0 0.1 dynamic_slice.7
  29.1 0.1 compare_select_fusion
  29.2 15.3 %collective-permute-done = f16[4,160,512]{2,1,0:T(8,128)(2,1)S(1)} collective-permute-done((f16[4,160,512]{2,1,0:T(8,128)(2,1)S(1)}, f16[4,160,512]{2,1,0:T(8,128)(2,1)S(1)}, u32[]{:S(2)}, u32[]{:S(2)}) %collective-permute-start) | collective-permute-done | bytes 655392 | tf_op jit(solution)/shard_map/ppermute | solution.py:16
  44.5 0.0 copy-done.1
  44.5 0.3 multiply_convert_fusion
  44.7 1.0 %collective-permute-start.1 = (bf16[4,160,512]{2,1,0:T(8,128)(2,1)S(1)}, bf16[4,160,512]{2,1,0:T(8,128)(2,1)S(1)}, u32[]{:S(2)}, u32[]{:S(2)}) collective-permute-start(bf16[4,160,512]{2,1,0:T(8,128)(2,1)S(1)} %multiply_convert_fusion), channel_id=1, source_target_pairs={{0,1},{1,0},{2,3},{3,2},{4,5},{5,4},{6,7},{7,6},{8,9},{9,8},{10,11... | collective-permute-start | bytes 1966088 | tf_op jit(solution)/shard_map/ppermute | solution.py:16
  45.7 0.0 copy-done
  45.7 0.1 dynamic-slice_bitcast_fusion
  45.8 0.7 %copy.10.keep = s32[8,1]{1,0:T(8,128)} copy(s32[8,1]{0,1:T(1,128)S(1)} %dynamic-slice_bitcast_fusion) | data formatting | bytes 64 | tf_op jit(solution)/shard_map/broadcast_in_dim | solution.py:396
  46.5 1.0 %collective-permute-done.1 = bf16[4,160,512]{2,1,0:T(8,128)(2,1)S(1)} collective-permute-done((bf16[4,160,512]{2,1,0:T(8,128)(2,1)S(1)}, bf16[4,160,512]{2,1,0:T(8,128)(2,1)S(1)}, u32[]{:S(2)}, u32[]{:S(2)}) %collective-permute-start.1) | collective-permute-done | bytes 655392 | tf_op jit(solution)/shard_map/ppermute | solution.py:16
  47.5 0.1 broadcast_select_fusion.1
  47.6 1.2 %pad_maximum_fusion.spectra = bf16[4,320,512]{2,1,0:T(8,128)(2,1)} fusion(bf16[4,160,512]{2,1,0:T(8,128)(2,1)S(1)} %get-tuple-element.10, bf16[4,160,512]{2,1,0:T(8,128)(2,1)S(1)} %get-tuple-element.9), kind=kLoop, calls=%fused_computation | loop fusion | flops 2621440 | bytes 2621440 | tf_op jit(solution)/shard_map/concatenate | solution.py:380
  48.7 6.7 %merge.1 = f32[5,32,8,1024]{3,2,1,0:T(8,128)} custom-call(s32[8,1]{1,0:T(8,128)} %copy.10.keep, bf16[4,320,512]{2,1,0:T(8,128)(2,1)} %pad_maximum_fusion.spectra, bf16[512,1024]{1,0:T(8,128)(2,1)} %get-tuple-element.11.table, f32[5,32,8,1024]{3,2,1,0:T(8,128)} %bitcast.12), custom_call_target="tpu_custom_call" | custom-call | tf_op jit(solution)/shard_map/merge/pallas_call | solution.py:384
  (4 shorter events, 0.0 us)
Async XLA Ops:
  0.0 45.7 %copy-start = (s32[64]{0:T(128)S(1)}, s32[64]{0:T(128)}, u32[]{:S(2)}) copy-start(s32[64]{0:T(128)} %param.6) | copy-start | bytes 772
  3.6 25.4 %copy-start.2 = (s32[64]{0:T(128)S(1)}, s32[64]{0:T(128)}, u32[]{:S(2)}) copy-start(s32[64]{0:T(128)} %param.7) | copy-start | bytes 772
  26.6 17.8 %copy-start.1 = (f32[4,160,512]{2,1,0:T(8,128)S(1)}, f32[4,160,512]{2,1,0:T(8,128)}, u32[]{:S(2)}) copy-start(f32[4,160,512]{2,1,0:T(8,128)} %get-tuple-element.7) | copy-start | bytes 3932164
  28.2 16.3 %collective-permute-start = (f16[4,160,512]{2,1,0:T(8,128)(2,1)S(1)}, f16[4,160,512]{2,1,0:T(8,128)(2,1)S(1)}, u32[]{:S(2)}, u32[]{:S(2)}) collective-permute-start(f16[4,160,512]{2,1,0:T(8,128)(2,1)S(1)} %convert_element_type.56), channel_id=1, source_target_pairs={{0,2},{1,3},{2,0},{3,1},{4,6},{5,7},{6,4},{7,5},{8,10},{9,11},{10,... | collective-permute-start | bytes 1966088 | tf_op jit(solution)/shard_map/ppermute | solution.py:16
  44.7 2.7 %collective-permute-start.1 = (bf16[4,160,512]{2,1,0:T(8,128)(2,1)S(1)}, bf16[4,160,512]{2,1,0:T(8,128)(2,1)S(1)}, u32[]{:S(2)}, u32[]{:S(2)}) collective-permute-start(bf16[4,160,512]{2,1,0:T(8,128)(2,1)S(1)} %multiply_convert_fusion), channel_id=1, source_target_pairs={{0,1},{1,0},{2,3},{3,2},{4,5},{5,4},{6,7},{7,6},{8,9},{9,8},{10,11... | collective-permute-start | bytes 1966088 | tf_op jit(solution)/shard_map/ppermute | solution.py:16

commit v4 on v3

--- a/solution.py
+++ b/solution.py
@@ -10,29 +10,13 @@
 KC = 256
 
 
-def flip(block, axis, bit):
-    count = lax.axis_size(axis)
-    route = [(i, i ^ (1 << bit)) for i in range(count) if i ^ (1 << bit) < count]
-    return lax.ppermute(block, axis, route)
-
-
-def angle_parts(columns, circle_size):
-    waves = jnp.arange(KC, dtype=jnp.int32)
-    product = columns[:, None] * waves[None, :] % circle_size
+def angle_parts(columns, circle_size, axis):
+    waves = lax.broadcasted_iota(
+        jnp.int32, (columns.size, KC) if axis == 1 else (KC, columns.size), axis
+    )
+    product = jnp.expand_dims(columns, axis) * waves % circle_size
     angles = product.astype(jnp.float32) * (2.0 * math.pi / circle_size)
     return jnp.cos(angles), jnp.sin(angles)
-
-
-def wave_table(first, column_count, circle_size):
-    fine = 32
-    coarse = column_count // fine
-    cos_c, sin_c = angle_parts(first + fine * jnp.arange(coarse, dtype=jnp.int32), circle_size)
-    cos_f, sin_f = angle_parts(jnp.arange(fine, dtype=jnp.int32), circle_size)
-    cos_c, sin_c = cos_c[:, None], sin_c[:, None]
-    cos_f, sin_f = cos_f[None], sin_f[None]
-    cosine = (cos_c * cos_f - sin_c * sin_f).astype(jnp.bfloat16).reshape(column_count, KC)
-    sine = (sin_c * cos_f + cos_c * sin_f).astype(jnp.bfloat16).reshape(column_count, KC)
-    return jnp.concatenate([cosine, sine], axis=1)
 
 
 def mode_scale(cutoffs, circle_size):
@@ -47,12 +31,17 @@
 def step_kernel(
     state,
     weights,
-    table,
+    cosines,
+    sines,
+    turned_cosines,
+    turned_sines,
+    scale,
+    keep,
     stepped,
-    totals,
     cells,
     planes,
     waves,
+    turned,
     results,
     rounded,
     top,
@@ -63,28 +52,38 @@
     columns_in,
     sides,
     partial,
-    arrived,
+    halves,
+    quarters,
+    half_in,
+    quarter_in,
+    spectra,
     load_sem,
-    table_sem,
     row_send,
     row_recv,
     side_send,
     side_recv,
     sum_send,
     sum_recv,
+    join_send,
+    join_recv,
     store_sem,
 ):
     chunks, fields, depth, columns = cells.shape
     size = top.shape[2]
     rows = depth // size
+    modes = waves.shape[1] // 2
     half = partial.shape[1] // 2
+    quarter = half // 2
     lat_count, lon_count = lax.axis_size("lat"), lax.axis_size("lon")
     lat, lon = lax.axis_index("lat"), lax.axis_index("lon")
     after = lax.rem(lon + 1, lon_count)
     before = lax.rem(lon + lon_count - 1, lon_count)
     across = lax.rem(lon + lon_count // 2, lon_count)
-    odd = lax.rem(lon, 2)
-    twin = lon + 1 - 2 * odd
+    bits = lon_count.bit_length() - 1
+    digit = [lax.rem(lon // (1 << b), 2) for b in range(bits)]
+    peer = [lon + (1 << b) - (2 << b) * digit[b] for b in range(bits)]
+    own_half = digit[0] * half
+    own_quarter = digit[1] * quarter
 
     def load(g):
         part = pl.ds(pl.multiple_of(g * depth, depth), depth)
@@ -121,21 +120,32 @@
             columns_out.at[k], columns_in.at[k], side_send.at[k], side_recv.at[k], device
         )
 
-    def sum_copy(g):
-        away = pl.ds(pl.multiple_of((1 - odd) * half, 8), half)
-        return remote(
-            partial.at[g, away], arrived.at[g], sum_send.at[g], sum_recv.at[g], (lat, twin)
-        )
+    def sum_copy(b, g):
+        if b == 0:
+            away = pl.ds(pl.multiple_of((1 - digit[0]) * half, 16), half)
+            source, target = partial.at[g, away], half_in.at[g]
+        elif b == 1:
+            away = pl.ds(pl.multiple_of((1 - digit[1]) * quarter, 16), quarter)
+            source, target = halves.at[g, away], quarter_in.at[0, g]
+        else:
+            source, target = quarters.at[b - 2, g], quarter_in.at[b - 1, g]
+        return remote(source, target, sum_send.at[b, g], sum_recv.at[b, g], (lat, peer[b]))
+
+    def join_copy(b, g):
+        if b == 0:
+            part = pl.ds(pl.multiple_of(own_half, 16), half)
+        else:
+            part = pl.ds(pl.multiple_of(own_half + own_quarter, 16), quarter)
+        view = spectra.at[g, part]
+        return remote(view, view, join_send.at[b, g], join_recv.at[b, g], (lat, peer[b]))
 
     for g in range(chunks):
         load(g)[0].start()
     for g in range(chunks):
         load(g)[1].start()
-    fetch_table = pltpu.make_async_copy(table, waves, table_sem)
-    fetch_table.start()
 
     barrier = pltpu.get_barrier_semaphore()
-    for other in (after, before, across, twin):
+    for other in (after, before, across, *peer):
         pl.semaphore_signal(barrier, inc=1, device_id=(lat, other), device_id_type=MESH)
 
     @pl.when(lat > 0)
@@ -150,11 +160,11 @@
 
     @pl.when(inside)
     def _():
-        pl.semaphore_wait(barrier, 6)
+        pl.semaphore_wait(barrier, 5 + bits)
 
     @pl.when(jnp.logical_not(inside))
     def _():
-        pl.semaphore_wait(barrier, 5)
+        pl.semaphore_wait(barrier, 4 + bits)
 
     taker = lax.broadcasted_iota(jnp.int32, (2 * size, depth), 0)
     taken = lax.broadcasted_iota(jnp.int32, (2 * size, depth), 1)
@@ -214,6 +224,26 @@
     pick(1, pl.ds(0, 128), 0)
     side_copy(1, (lat, before)).start()
 
+    fine = 32
+    coarse = columns // fine
+    fine_cos, fine_sin = cosines[coarse:], sines[coarse:]
+
+    def fill(at, carry):
+        span = pl.ds(pl.multiple_of(at * fine, fine), fine)
+        coarse_cos, coarse_sin = cosines[pl.ds(at, 1)], sines[pl.ds(at, 1)]
+        waves[span, :modes] = (coarse_cos * fine_cos - coarse_sin * fine_sin).astype(jnp.bfloat16)
+        waves[span, modes:] = (coarse_sin * fine_cos + coarse_cos * fine_sin).astype(jnp.bfloat16)
+        return carry
+
+    lax.fori_loop(0, coarse, fill, 0)
+    lane_cos, lane_sin = turned_cosines[:, :128], turned_sines[:, :128]
+    for at in range(columns // 128):
+        span = pl.ds(at * 128, 128)
+        tile_cos = turned_cosines[:, 128 + at : 129 + at]
+        tile_sin = turned_sines[:, 128 + at : 129 + at]
+        turned[:modes, span] = (tile_cos * lane_cos - tile_sin * lane_sin).astype(jnp.bfloat16)
+        turned[modes:, span] = (tile_sin * lane_cos + tile_cos * lane_sin).astype(jnp.bfloat16)
+
     spread = jnp.where(line == 0, 1.0, 0.0).astype(jnp.bfloat16)
     for k in range(2):
         side_copy(k, (lat, after)).wait_recv()
@@ -224,13 +254,12 @@
                 (((0,), (0,)), ((), ())),
                 preferred_element_type=jnp.float32,
             )
-    fetch_table.wait()
 
     lane = lax.broadcasted_iota(jnp.int32, (rows, columns), 1)
     level_line = lax.broadcasted_iota(jnp.int32, (rows, columns), 0)
     copies = columns // 128
 
-    def one_chunk(g, carry):
+    def advance(g):
         load(g)[1].wait()
         row_copy(g, True, (lat, across), True).wait_recv()
         row_copy(g, False, (lat, across), False).wait_recv()
@@ -267,23 +296,77 @@
             return inner
 
         lax.fori_loop(0, fields, one_field, 0)
+        partial[g] = jnp.dot(rounded[...], waves[...], preferred_element_type=jnp.float32)
+        sum_copy(0, g).start()
+
+    def pair_sum(g):
+        sum_copy(0, g).wait_recv()
+        mine = pl.ds(pl.multiple_of(own_half, 16), half)
+        halves[g] = partial[g, mine] + half_in[g]
+        sum_copy(1, g).start()
+
+    def full_sum(g):
+        sum_copy(1, g).wait_recv()
+        mine = pl.ds(pl.multiple_of(own_quarter, 16), quarter)
+        total = halves[g, mine] + quarter_in[0, g]
+        for b in range(2, bits):
+            quarters[b - 2, g] = total
+            sum_copy(b, g).start()
+            sum_copy(b, g).wait_recv()
+            total = total + quarter_in[b - 1, g]
+        scaled = total.reshape(quarter // rows, rows, 2 * modes) * scale[...]
+        part = pl.ds(pl.multiple_of(own_half + own_quarter, 16), quarter)
+        spectra[g, part] = scaled.reshape(quarter, 2 * modes).astype(jnp.bfloat16)
+        join_copy(1, g).start()
+
+    def join(g):
+        join_copy(1, g).wait_recv()
+        join_copy(0, g).start()
+
+    def merge(g):
+        join_copy(0, g).wait_recv()
+        smooth = jnp.dot(spectra[g], turned[...], preferred_element_type=jnp.float32)
+        smooth = smooth.astype(jnp.bfloat16).astype(jnp.float32)
+        smooth = smooth.reshape(fields, size, rows, columns)
+        kept = jnp.broadcast_to(keep[...], (rows, columns)) != 0
+        for field in range(fields):
+            for at in range(size):
+                span = pl.ds(at * rows, rows)
+                results[g, field, span] = jnp.where(
+                    kept, smooth[field, at], results[g, field, span]
+                )
         store(g).start()
-        partial[g] = jnp.dot(rounded[...], waves[...], preferred_element_type=jnp.float32)
-        sum_copy(g).start()
+
+    def phase(t, carry):
+        @pl.when(t < chunks)
+        def _():
+            advance(t)
+
+        @pl.when((t >= 1) & (t <= chunks))
+        def _():
+            full_sum(t - 1)
+
+        @pl.when(t >= 3)
+        def _():
+            merge(t - 3)
+
+        @pl.when((t >= 2) & (t <= chunks + 1))
+        def _():
+            join(t - 2)
+
+        @pl.when(t < chunks)
+        def _():
+            pair_sum(t)
+
         return carry
 
-    lax.fori_loop(0, chunks, one_chunk, 0)
-
-    def one_total(g, carry):
-        sum_copy(g).wait_recv()
-        mine = pl.ds(pl.multiple_of(odd * half, 8), half)
-        totals[g] = partial[g, mine] + arrived[g]
-        return carry
-
-    lax.fori_loop(0, chunks, one_total, 0)
+    lax.fori_loop(0, chunks + 3, phase, 0)
 
     def finish(g, carry):
-        sum_copy(g).wait_send()
+        for b in range(bits):
+            sum_copy(b, g).wait_send()
+        for b in range(2):
+            join_copy(b, g).wait_send()
         row_copy(g, True, (lat, across), True).wait_send()
         row_copy(g, False, (lat, across), False).wait_send()
         store(g).wait()
@@ -292,23 +375,6 @@
     lax.fori_loop(0, chunks, finish, 0)
     for k in range(2):
         side_copy(k, (lat, after)).wait_send()
-
-
-def merge_kernel(keep, spectra, table, stepped, merged):
-    fields, levels, rows, columns = stepped.shape
-    smooth = jnp.dot(spectra[0], table[...], preferred_element_type=jnp.float32)
-    smooth = smooth.astype(jnp.bfloat16).astype(jnp.float32)
-    smooth = smooth.reshape(fields, levels, rows, columns)
-    kept = jnp.broadcast_to(keep[...], (rows, columns)) != 0
-    merged[...] = jnp.where(kept, smooth, stepped[...])
-
-
-def chunk_of(fields, levels, rows, columns, size):
-    return pl.BlockSpec((fields, size, rows, columns), lambda i: (0, i, 0, 0))
-
-
-def whole(*shape):
-    return pl.BlockSpec(shape, lambda i: (0,) * len(shape), pipeline_mode=pl.Buffered(1))
 
 
 def on_device(state_fields, stencil_weights, filter_mask, cutoff_wave):
@@ -316,31 +382,46 @@
     lat_count, lon_count = lax.axis_size("lat"), lax.axis_size("lon")
     lat_pos, lon_pos = lax.axis_index("lat"), lax.axis_index("lon")
     circle_size = columns * lon_count
-    bits = lon_count.bit_length() - 1
     size = 8
     steps = levels // size
     start = lat_pos * rows
     cuts = lax.dynamic_slice_in_dim(cutoff_wave, start, rows)
     mask = lax.dynamic_slice_in_dim(filter_mask, start, rows)
-    table = wave_table(lon_pos * columns, columns, circle_size)
+    scale = mode_scale(cuts, circle_size)
+    origin = lon_pos * columns
+    cosines, sines = angle_parts(
+        jnp.concatenate(
+            [origin + 32 * jnp.arange(columns // 32), jnp.arange(32)]
+        ).astype(jnp.int32),
+        circle_size,
+        1,
+    )
+    turned_cosines, turned_sines = angle_parts(
+        jnp.concatenate(
+            [jnp.arange(128), origin + 128 * jnp.arange(columns // 128)]
+        ).astype(jnp.int32),
+        circle_size,
+        0,
+    )
     rows_each = fields * size * rows
     depth = size * rows
     anywhere = pl.BlockSpec(memory_space=pl.ANY)
     dma = pltpu.SemaphoreType.DMA
     strip = pltpu.VMEM((steps, fields, size, columns), jnp.bfloat16)
     column_strip = pltpu.VMEM((2, steps * fields, 16, depth), jnp.bfloat16)
-    stepped, total = pl.pallas_call(
+    extra = max(lon_count.bit_length() - 3, 1)
+    in_vmem = pl.BlockSpec(memory_space=pltpu.VMEM)
+    bits = lon_count.bit_length() - 1
+    advanced = pl.pallas_call(
         step_kernel,
-        in_specs=[anywhere] * 3,
-        out_specs=[anywhere, pl.BlockSpec(memory_space=pltpu.VMEM)],
-        out_shape=[
-            jax.ShapeDtypeStruct((fields, levels * rows, columns), jnp.float32),
-            jax.ShapeDtypeStruct((steps, rows_each // 2, 2 * KC), jnp.float32),
-        ],
+        in_specs=[anywhere] * 2 + [in_vmem] * 6,
+        out_specs=anywhere,
+        out_shape=jax.ShapeDtypeStruct((fields, levels * rows, columns), jnp.float32),
         scratch_shapes=[
             pltpu.VMEM((steps, fields, depth, columns), jnp.float32),
             pltpu.VMEM((steps, 4, depth, columns), jnp.float32),
             pltpu.VMEM((columns, 2 * KC), jnp.bfloat16),
+            pltpu.VMEM((2 * KC, columns), jnp.bfloat16),
             pltpu.VMEM((steps, fields, depth, columns), jnp.float32),
             pltpu.VMEM((rows_each, columns), jnp.bfloat16),
             strip,
@@ -352,48 +433,36 @@
             pltpu.VMEM((2, steps * fields, depth, 128), jnp.float32),
             pltpu.VMEM((steps, rows_each, 2 * KC), jnp.float32),
             pltpu.VMEM((steps, rows_each // 2, 2 * KC), jnp.float32),
+            pltpu.VMEM((extra, steps, rows_each // 4, 2 * KC), jnp.float32),
+            pltpu.VMEM((steps, rows_each // 2, 2 * KC), jnp.float32),
+            pltpu.VMEM((bits - 1, steps, rows_each // 4, 2 * KC), jnp.float32),
+            pltpu.VMEM((steps, rows_each, 2 * KC), jnp.bfloat16),
             dma((2, steps)),
-            dma,
             dma((2, steps)),
             dma((2, steps)),
             dma((2,)),
             dma((2,)),
-            dma((steps,)),
-            dma((steps,)),
+            dma((bits, steps)),
+            dma((bits, steps)),
+            dma((2, steps)),
+            dma((2, steps)),
             dma((steps,)),
         ],
-        compiler_params=pltpu.CompilerParams(collective_id=0, has_side_effects=True),
+        compiler_params=pltpu.CompilerParams(
+            collective_id=0, has_side_effects=True, vmem_limit_bytes=60 << 20
+        ),
         name="step",
     )(
         state_fields.reshape(fields, levels * rows, columns),
         stencil_weights.reshape(4, levels * rows, columns),
-        table,
+        cosines,
+        sines,
+        turned_cosines,
+        turned_sines,
+        scale,
+        mask[:, None],
     )
-    stepped = stepped.reshape(state_fields.shape)
-    low = lon_pos % 2 == 0
-    for bit in range(1, bits):
-        total = total + flip(total.astype(jnp.float16), "lon", bit).astype(jnp.float32)
-    scale = mode_scale(cuts, circle_size)
-    spectra = (total.reshape(steps, -1, rows, 2 * KC) * scale).astype(jnp.bfloat16)
-    spectra = spectra.reshape(steps, -1, 2 * KC)
-    other = flip(spectra, "lon", 0)
-    spectra = jnp.concatenate(
-        [jnp.where(low, spectra, other), jnp.where(low, other, spectra)], axis=1
-    )
-    back_table = table.T
-    return pl.pallas_call(
-        merge_kernel,
-        grid=(steps,),
-        in_specs=[
-            whole(rows, 1),
-            pl.BlockSpec((1, rows_each, 2 * KC), lambda i: (i, 0, 0)),
-            whole(2 * KC, columns),
-            chunk_of(fields, levels, rows, columns, size),
-        ],
-        out_specs=chunk_of(fields, levels, rows, columns, size),
-        out_shape=jax.ShapeDtypeStruct(state_fields.shape, jnp.float32),
-        name="merge",
-    )(mask[:, None], spectra, back_table, stepped)
+    return advanced.reshape(state_fields.shape)
 
 
 def solution(mesh):

time: 55.7 us -> 61.7 us (1.11)
  Pallas kernels: 29.8 us -> 50.1 us
  waiting for transfers between devices: 16.2 us -> 0 us
  local copies, waits for them, and re-layouts: 2.59 us -> 7.83 us
  starting transfers between devices: 1.82 us -> 0 us
  other arithmetic: 4.98 us -> 3.57 us
    pallas_call x2 -> x1, Pallas kernels: 29.8 us -> 50.1 us  [on_device(): pl.pallas_call(step_kernel, in_specs=[anywhere] * 2 + [in_vmem] * 6, out_...]
    ppermute x2 -> x0, waiting for transfers between devices: 16.2 us -> none  [flip(): return lax.ppermute(block, axis, route)]
    unnamed x6 -> x3, local copies, waits for them, and re-layouts: 0.01 us -> 6.35 us
    sin x1 -> x2, other arithmetic: 0.14 us -> 2.8 us  [angle_parts(): return (jnp.cos(angles), jnp.sin(angles))]
    convert_element_type x3 -> x0, other arithmetic: 2.16 us -> none  [the longest x1 1.54 us: on_device(): total.astype(jnp.float16)]
    ppermute x2 -> x0, starting transfers between devices: 1.82 us -> none  [flip(): return lax.ppermute(block, axis, route)]
    concatenate x1 -> x0, local copies, waits for them, and re-layouts: 1.32 us -> none  [wave_table(): return jnp.concatenate([cosine, sine], axis=1)]
    concatenate x1 -> x2, other arithmetic: 1.19 us -> 0.09 us  [the longest x1 0.08 us: on_device(): jnp.concatenate([origin + 32 * jnp.arange(columns // 32), jnp.arange(32)])]
  transfers between devices with their start and end apart: 2 -> 0, of which waited for: 2 -> 0; matrix products, arithmetic and copies ran while one was open for 2% -> 0% of each run, Pallas kernels for 0% -> 0%
where the time goes in v4:
time: 61.7 us; the launch traced here: 61.5 us
  Pallas kernels  50.1 us (81%)
  local copies, waits for them, and re-layouts  7.83 us (13%)
  other arithmetic  3.57 us (6%)
    pallas_call x1, Pallas kernels, on_device(): pl.pallas_call(step_kernel, in_specs=[anywhere] * 2 + [in_vmem] * 6, out_...  50.1 us
    unnamed x3, local copies, waits for them, and re-layouts  6.35 us
    sin x2, other arithmetic, angle_parts(): return (jnp.cos(angles), jnp.sin(angles))  2.8 us

profile of v4, /device:TPU:9, one launch (start us, length us, event | category | flops | bytes accessed | tf_op | source)
XLA Modules:
  0.0 61.5 jit_solution(2596697256067650421)
XLA Ops:
  0.0 0.0 copy-start
  0.0 0.7 %copy-done = s32[64]{0:T(128)S(1)} copy-done((s32[64]{0:T(128)S(1)}, s32[64]{0:T(128)}, u32[]{:S(2)}) %copy-start) | copy-done | bytes 280
  0.7 0.1 dynamic-slice_bitcast_fusion
  0.7 0.7 %dynamic_slice.6 = s32[8]{0:T(128)S(1)} dynamic-slice(s32[64]{0:T(128)} %param.7, s32[]{:T(128)S(6)} %select_n.47), dynamic_slice_sizes={8} | dynamic-slice | bytes 68 | tf_op jit(solution)/shard_map/dynamic_slice | solution.py:388
  1.5 0.1 pad_add_fusion.1
  1.6 0.7 %copy.5.keep = s32[8,1]{1,0:T(8,128)} copy(s32[8,1]{0,1:T(1,128)S(1)} %dynamic-slice_bitcast_fusion) | data formatting | bytes 64 | tf_op jit(solution)/shard_map/broadcast_in_dim | solution.py:463
  2.3 0.7 %compare_select_fusion.scale = f32[8,512]{1,0:T(8,128)} fusion(f32[512]{0:T(512)S(1)} %compare_select_fusion.1, s32[512]{0:T(512)S(1)} %add_select_fusion.2, s32[8]{0:T(128)S(1)} %dynamic_slice.6), kind=kLoop, calls=%fused_computation.22 | loop fusion | flops 8192 | bytes 20512 | tf_op jit(solution)/shard_map/jit(_where)/select_n | solution.py:25
  2.9 1.0 %fusion.14 = (f32[64,256]{1,0:T(8,128)}, f32[64,256]{1,0:T(8,128)}) fusion(s32[64]{0:T(128)S(1)} %pad_add_fusion.1), kind=kLoop, calls=%fused_computation.20 | loop fusion | flops 229376 | bytes 131328 | tf_op jit(solution)/shard_map/sin | solution.py:19
  3.9 1.8 %fusion.6 = (f32[256,136]{1,0:T(8,128)}, f32[256,136]{1,0:T(8,128)}) fusion(s32[136]{0:T(256)S(1)} %pad_add_fusion), kind=kLoop, calls=%fused_computation.9 | loop fusion | flops 487424 | bytes 279072 | tf_op jit(solution)/shard_map/sin | solution.py:19
  5.7 50.1 %step.1 = f32[5,256,1024]{2,1,0:T(8,128)} custom-call(f32[5,256,1024]{2,1,0:T(8,128)} %bitcast.6, f32[4,256,1024]{2,1,0:T(8,128)} %bitcast.7, f32[64,256]{1,0:T(8,128)} %get-tuple-element.8.cosines, f32[64,256]{1,0:T(8,128)} %get-tuple-element.7.sines, f32[256,136]{1,0:T(8,128)} %get-tuple-element.6.turned_cosines, ...), custom_call_target="tpu_custom_call" | custom-call | tf_op jit(solution)/shard_map/step/pallas_call | solution.py:415
  55.8 5.7 %copy.7 = f32[5,32,8,1024]{3,2,1,0:T(8,128)} copy(f32[5,32,8,1024]{3,2,1,0:T(8,128)} %bitcast.5) | data formatting | bytes 10485760
  (7 shorter events, 0.0 us)
Async XLA Ops:
  0.0 0.7 %copy-start = (s32[64]{0:T(128)S(1)}, s32[64]{0:T(128)}, u32[]{:S(2)}) copy-start(s32[64]{0:T(128)} %param.6) | copy-start | bytes 772

commit v5 on v4

--- a/solution.py
+++ b/solution.py
@@ -19,12 +19,6 @@
     return jnp.cos(angles), jnp.sin(angles)
 
 
-def mode_scale(cutoffs, circle_size):
-    waves = jnp.arange(2 * KC, dtype=jnp.int32) % KC
-    weights = jnp.where(waves == 0, 1.0 / circle_size, 2.0 / circle_size).astype(jnp.float32)
-    return jnp.where(waves[None, :] <= cutoffs[:, None], weights[None, :], jnp.float32(0.0))
-
-
 MESH = pl.DeviceIdType.MESH
 
 
@@ -35,8 +29,7 @@
     sines,
     turned_cosines,
     turned_sines,
-    scale,
-    keep,
+    bounds,
     stepped,
     cells,
     planes,
@@ -259,6 +252,11 @@
     level_line = lax.broadcasted_iota(jnp.int32, (rows, columns), 0)
     copies = columns // 128
 
+    wave = lax.rem(lax.broadcasted_iota(jnp.int32, (rows, 2 * modes), 1), modes)
+    circle_size = columns * lon_count
+    weight = jnp.where(wave == 0, 1.0 / circle_size, 2.0 / circle_size)
+    scale = jnp.where(wave <= bounds[:, 1:2], weight, 0.0).astype(jnp.float32)
+
     def advance(g):
         load(g)[1].wait()
         row_copy(g, True, (lat, across), True).wait_recv()
@@ -314,7 +312,7 @@
             sum_copy(b, g).start()
             sum_copy(b, g).wait_recv()
             total = total + quarter_in[b - 1, g]
-        scaled = total.reshape(quarter // rows, rows, 2 * modes) * scale[...]
+        scaled = total.reshape(quarter // rows, rows, 2 * modes) * scale[None]
         part = pl.ds(pl.multiple_of(own_half + own_quarter, 16), quarter)
         spectra[g, part] = scaled.reshape(quarter, 2 * modes).astype(jnp.bfloat16)
         join_copy(1, g).start()
@@ -328,7 +326,7 @@
         smooth = jnp.dot(spectra[g], turned[...], preferred_element_type=jnp.float32)
         smooth = smooth.astype(jnp.bfloat16).astype(jnp.float32)
         smooth = smooth.reshape(fields, size, rows, columns)
-        kept = jnp.broadcast_to(keep[...], (rows, columns)) != 0
+        kept = jnp.broadcast_to(bounds[:, 0:1], (rows, columns)) != 0
         for field in range(fields):
             for at in range(size):
                 span = pl.ds(at * rows, rows)
@@ -337,30 +335,41 @@
                 )
         store(g).start()
 
-    def phase(t, carry):
-        @pl.when(t < chunks)
-        def _():
-            advance(t)
-
-        @pl.when((t >= 1) & (t <= chunks))
-        def _():
-            full_sum(t - 1)
-
-        @pl.when(t >= 3)
-        def _():
-            merge(t - 3)
-
-        @pl.when((t >= 2) & (t <= chunks + 1))
-        def _():
-            join(t - 2)
-
-        @pl.when(t < chunks)
-        def _():
-            pair_sum(t)
-
-        return carry
-
-    lax.fori_loop(0, chunks + 3, phase, 0)
+    def forward(t, carry):
+        advance(t)
+
+        @pl.when(t >= 1)
+        def _():
+            pair_sum(t - 1)
+
+        return carry
+
+    last = chunks - 1
+    lax.fori_loop(0, chunks, forward, 0)
+    full_sum(0)
+    pair_sum(last)
+
+    def sums(g, carry):
+        full_sum(g)
+        return carry
+
+    def joins(g, carry):
+        join(g)
+        return carry
+
+    def merges(g, carry):
+        merge(g)
+
+        @pl.when(g + 2 < chunks)
+        def _():
+            join(g + 2)
+
+        return carry
+
+    lax.fori_loop(1, last, sums, 0)
+    lax.fori_loop(0, 2, joins, 0)
+    full_sum(last)
+    lax.fori_loop(0, chunks, merges, 0)
 
     def finish(g, carry):
         for b in range(bits):
@@ -385,9 +394,7 @@
     size = 8
     steps = levels // size
     start = lat_pos * rows
-    cuts = lax.dynamic_slice_in_dim(cutoff_wave, start, rows)
-    mask = lax.dynamic_slice_in_dim(filter_mask, start, rows)
-    scale = mode_scale(cuts, circle_size)
+    bounds = lax.dynamic_slice_in_dim(jnp.stack([filter_mask, cutoff_wave], axis=1), start, rows)
     origin = lon_pos * columns
     cosines, sines = angle_parts(
         jnp.concatenate(
@@ -414,7 +421,7 @@
     bits = lon_count.bit_length() - 1
     advanced = pl.pallas_call(
         step_kernel,
-        in_specs=[anywhere] * 2 + [in_vmem] * 6,
+        in_specs=[anywhere] * 2 + [in_vmem] * 5,
         out_specs=anywhere,
         out_shape=jax.ShapeDtypeStruct((fields, levels * rows, columns), jnp.float32),
         scratch_shapes=[
@@ -449,7 +456,7 @@
             dma((steps,)),
         ],
         compiler_params=pltpu.CompilerParams(
-            collective_id=0, has_side_effects=True, vmem_limit_bytes=60 << 20
+            collective_id=0, has_side_effects=True, vmem_limit_bytes=38 << 20
         ),
         name="step",
     )(
@@ -459,8 +466,7 @@
         sines,
         turned_cosines,
         turned_sines,
-        scale,
-        mask[:, None],
+        bounds,
     )
     return advanced.reshape(state_fields.shape)
 

time: 61.7 us -> 52.9 us (0.86)
  Pallas kernels: 50.1 us -> 43.3 us
  other arithmetic: 3.57 us -> 2.15 us
  local copies, waits for them, and re-layouts: 7.83 us -> 7.19 us
    pallas_call x1, Pallas kernels: 50.1 us -> 43.3 us  [on_device(): pl.pallas_call(step_kernel, in_specs=[anywhere] * 2 + [in_vmem] * 5, out_...]
    sin x2, other arithmetic: 2.8 us -> 1.37 us  [angle_parts(): return (jnp.cos(angles), jnp.sin(angles))]
    unnamed x3 -> x6, local copies, waits for them, and re-layouts: 6.35 us -> 7.11 us
    broadcast_in_dim x2 -> x0, local copies, waits for them, and re-layouts: 0.74 us -> none  [on_device(): mask[:, None]]
    another operation x0 -> x1, other arithmetic: none -> 0.68 us  [on_device(): jnp.stack([filter_mask, cutoff_wave], axis=1)]
    select_n x3 -> x0, other arithmetic: 0.67 us -> none  [the longest x1 0.67 us: mode_scale(): jnp.where(waves[None, :] <= cutoffs[:, None], weights[None, :], jnp.float...]
    dynamic_slice x1, local copies, waits for them, and re-layouts: 0.73 us -> 0.07 us  [on_device(): lax.dynamic_slice_in_dim(jnp.stack([filter_mask, cutoff_wave], axis=1), s...]
where the time goes in v5:
time: 52.9 us; the launch traced here: 52.7 us
  Pallas kernels  43.3 us (82%)
  local copies, waits for them, and re-layouts  7.19 us (14%)
  other arithmetic  2.15 us (4%)
    pallas_call x1, Pallas kernels, on_device(): pl.pallas_call(step_kernel, in_specs=[anywhere] * 2 + [in_vmem] * 5, out_...  43.3 us
    unnamed x6, local copies, waits for them, and re-layouts  7.11 us
    sin x2, other arithmetic, angle_parts(): return (jnp.cos(angles), jnp.sin(angles))  1.37 us

profile of v5, /device:TPU:9, one launch (start us, length us, event | category | flops | bytes accessed | tf_op | source)
XLA Modules:
  0.0 52.7 jit_solution(13141997643848290129)
XLA Ops:
  0.0 0.1 pad_add_fusion.2
  0.1 0.7 %pad_add_fusion.1 = s32[64,2]{0,1:T(2,128)S(1)} fusion(s32[64,1]{0,1:T(1,128)} %bitcast.8, s32[64,1]{0,1:T(1,128)} %bitcast.9), kind=kLoop, calls=%fused_computation.23 | loop fusion | flops 128 | bytes 1024 | tf_op jit(solution)/shard_map/stack | solution.py:397
  0.8 0.1 constant_dynamic-slice_fusion
  0.9 0.1 copy.8.bounds
  1.0 0.3 fusion.14
  1.3 1.0 %fusion.6 = (f32[256,136]{1,0:T(8,128)S(1)}, f32[256,136]{1,0:T(8,128)S(1)}) fusion(s32[136]{0:T(256)S(1)} %pad_add_fusion), kind=kLoop, calls=%fused_computation.9 | loop fusion | flops 487424 | bytes 279072 | tf_op jit(solution)/shard_map/sin | solution.py:19
  2.3 0.0 copy-start
  2.4 2.5 %copy-done = f32[5,32,8,1024]{3,2,1,0:T(8,128)S(1)} copy-done((f32[5,32,8,1024]{3,2,1,0:T(8,128)S(1)}, f32[5,32,8,1024]{3,2,1,0:T(8,128)}, u32[]{:S(2)}) %copy-start) | copy-done | bytes 5242904
  4.8 0.0 copy-start.1
  4.8 2.2 %copy-done.1 = f32[4,32,8,1024]{3,2,1,0:T(8,128)S(1)} copy-done((f32[4,32,8,1024]{3,2,1,0:T(8,128)S(1)}, f32[4,32,8,1024]{3,2,1,0:T(8,128)}, u32[]{:S(2)}) %copy-start.1) | copy-done | bytes 4194328
  7.0 43.3 %step.1 = f32[5,256,1024]{2,1,0:T(8,128)S(1)} custom-call(f32[5,256,1024]{2,1,0:T(8,128)S(1)} %bitcast.6, f32[4,256,1024]{2,1,0:T(8,128)S(1)} %bitcast.7, f32[64,256]{1,0:T(8,128)S(1)} %get-tuple-element.8.cosines, f32[64,256]{1,0:T(8,128)S(1)} %get-tuple-element.7.sines, f32[256,136]{1,0:T(8,128)S(1)} %get-tuple-element.6.turned_cosines, ...), custom_call_target="tpu_custom_call" | custom-call | tf_op jit(solution)/shard_map/step/pallas_call | solution.py:422
  50.3 2.4 %copy.10 = f32[5,32,8,1024]{3,2,1,0:T(8,128)} copy(f32[5,32,8,1024]{3,2,1,0:T(8,128)S(1)} %bitcast.5) | data formatting | bytes 10485760
  (5 shorter events, 0.0 us)
Async XLA Ops:
  2.3 2.5 %copy-start = (f32[5,32,8,1024]{3,2,1,0:T(8,128)S(1)}, f32[5,32,8,1024]{3,2,1,0:T(8,128)}, u32[]{:S(2)}) copy-start(f32[5,32,8,1024]{3,2,1,0:T(8,128)} %param.4) | copy-start | bytes 15728644
  4.8 2.2 %copy-start.1 = (f32[4,32,8,1024]{3,2,1,0:T(8,128)S(1)}, f32[4,32,8,1024]{3,2,1,0:T(8,128)}, u32[]{:S(2)}) copy-start(f32[4,32,8,1024]{3,2,1,0:T(8,128)} %param.5) | copy-start | bytes 12582916

commit v6 on v5

--- a/solution.py
+++ b/solution.py
@@ -30,12 +30,9 @@
     turned_cosines,
     turned_sines,
     bounds,
-    stepped,
-    cells,
-    planes,
+    results,
     waves,
     turned,
-    results,
     rounded,
     top,
     bottom,
@@ -50,7 +47,6 @@
     half_in,
     quarter_in,
     spectra,
-    load_sem,
     row_send,
     row_recv,
     side_send,
@@ -59,10 +55,10 @@
     sum_recv,
     join_send,
     join_recv,
-    store_sem,
 ):
-    chunks, fields, depth, columns = cells.shape
-    size = top.shape[2]
+    fields, lines, columns = state.shape
+    chunks, _, size, _ = top.shape
+    depth = lines // chunks
     rows = depth // size
     modes = waves.shape[1] // 2
     half = partial.shape[1] // 2
@@ -78,16 +74,8 @@
     own_half = digit[0] * half
     own_quarter = digit[1] * quarter
 
-    def load(g):
-        part = pl.ds(pl.multiple_of(g * depth, depth), depth)
-        return (
-            pltpu.make_async_copy(state.at[:, part], cells.at[g], load_sem.at[0, g]),
-            pltpu.make_async_copy(weights.at[:, part], planes.at[g], load_sem.at[1, g]),
-        )
-
-    def store(g):
-        part = pl.ds(pl.multiple_of(g * depth, depth), depth)
-        return pltpu.make_async_copy(results.at[g], stepped.at[:, part], store_sem.at[g])
+    def span_of(g, first, count):
+        return pl.ds(pl.multiple_of(g * depth + first, count), count)
 
     def remote(source, target, sent, got, device):
         return pltpu.make_async_remote_copy(
@@ -132,11 +120,6 @@
         view = spectra.at[g, part]
         return remote(view, view, join_send.at[b, g], join_recv.at[b, g], (lat, peer[b]))
 
-    for g in range(chunks):
-        load(g)[0].start()
-    for g in range(chunks):
-        load(g)[1].start()
-
     barrier = pltpu.get_barrier_semaphore()
     for other in (after, before, across, *peer):
         pl.semaphore_signal(barrier, inc=1, device_id=(lat, other), device_id_type=MESH)
@@ -165,14 +148,13 @@
     gather = jnp.where(taken == wanted, 1.0, 0.0).astype(jnp.bfloat16)
 
     def send_rows(g, carry):
-        load(g)[0].wait()
         for field in range(fields):
             sign = -1.0 if field < 2 else 1.0
             up_sign = jnp.where(lat == 0, sign, 1.0).astype(jnp.float32)
             down_sign = jnp.where(lat == lat_count - 1, sign, 1.0).astype(jnp.float32)
             edges = jnp.dot(
                 gather,
-                cells[g, field].astype(jnp.bfloat16),
+                state[field, span_of(g, 0, depth)].astype(jnp.bfloat16),
                 preferred_element_type=jnp.float32,
             )
             top[g, field] = (edges[:size] * up_sign).astype(jnp.bfloat16)
@@ -206,7 +188,7 @@
         for g in range(chunks):
             for field in range(0, fields):
                 first = (g * fields + field) * depth
-                edge = cells[g, field, :, lanes].astype(jnp.bfloat16)
+                edge = state[field, span_of(g, 0, depth), lanes].astype(jnp.bfloat16)
                 picked = lax.dot_general(
                     chosen, edge, (((1,), (1,)), ((), ())), preferred_element_type=jnp.float32
                 )
@@ -258,7 +240,6 @@
     scale = jnp.where(wave <= bounds[:, 1:2], weight, 0.0).astype(jnp.float32)
 
     def advance(g):
-        load(g)[1].wait()
         row_copy(g, True, (lat, across), True).wait_recv()
         row_copy(g, False, (lat, across), False).wait_recv()
 
@@ -269,7 +250,8 @@
                 pair = []
                 for at in (level, level + 1):
                     span = pl.ds(at * rows, rows)
-                    x = cells[g, field, span]
+                    here = span_of(g, at * rows, rows)
+                    x = state[field, here]
                     left = jnp.concatenate([sides[0, g * fields + field, span]] * copies, axis=1)
                     right = jnp.concatenate([sides[1, g * fields + field, span]] * copies, axis=1)
                     w = jnp.where(lane == 0, left, pltpu.roll(x, 1, 1))
@@ -280,12 +262,12 @@
                     )
                     y = (
                         x
-                        + planes[g, 0, span] * (e - x)
-                        + planes[g, 1, span] * (w - x)
-                        + planes[g, 2, span] * (n - x)
-                        + planes[g, 3, span] * (s - x)
+                        + weights[0, here] * (e - x)
+                        + weights[1, here] * (w - x)
+                        + weights[2, here] * (n - x)
+                        + weights[3, here] * (s - x)
                     )
-                    results[g, field, span] = y
+                    results[field, here] = y
                     pair.append(y)
                 first = pl.multiple_of(field * depth + level * rows, 2 * rows)
                 rounded[pl.ds(first, 2 * rows), :] = jnp.concatenate(pair, axis=0).astype(
@@ -329,11 +311,8 @@
         kept = jnp.broadcast_to(bounds[:, 0:1], (rows, columns)) != 0
         for field in range(fields):
             for at in range(size):
-                span = pl.ds(at * rows, rows)
-                results[g, field, span] = jnp.where(
-                    kept, smooth[field, at], results[g, field, span]
-                )
-        store(g).start()
+                here = span_of(g, at * rows, rows)
+                results[field, here] = jnp.where(kept, smooth[field, at], results[field, here])
 
     def forward(t, carry):
         advance(t)
@@ -378,7 +357,6 @@
             join_copy(b, g).wait_send()
         row_copy(g, True, (lat, across), True).wait_send()
         row_copy(g, False, (lat, across), False).wait_send()
-        store(g).wait()
         return carry
 
     lax.fori_loop(0, chunks, finish, 0)
@@ -412,7 +390,6 @@
     )
     rows_each = fields * size * rows
     depth = size * rows
-    anywhere = pl.BlockSpec(memory_space=pl.ANY)
     dma = pltpu.SemaphoreType.DMA
     strip = pltpu.VMEM((steps, fields, size, columns), jnp.bfloat16)
     column_strip = pltpu.VMEM((2, steps * fields, 16, depth), jnp.bfloat16)
@@ -421,15 +398,12 @@
     bits = lon_count.bit_length() - 1
     advanced = pl.pallas_call(
         step_kernel,
-        in_specs=[anywhere] * 2 + [in_vmem] * 5,
-        out_specs=anywhere,
+        in_specs=[in_vmem] * 7,
+        out_specs=in_vmem,
         out_shape=jax.ShapeDtypeStruct((fields, levels * rows, columns), jnp.float32),
         scratch_shapes=[
-            pltpu.VMEM((steps, fields, depth, columns), jnp.float32),
-            pltpu.VMEM((steps, 4, depth, columns), jnp.float32),
             pltpu.VMEM((columns, 2 * KC), jnp.bfloat16),
             pltpu.VMEM((2 * KC, columns), jnp.bfloat16),
-            pltpu.VMEM((steps, fields, depth, columns), jnp.float32),
             pltpu.VMEM((rows_each, columns), jnp.bfloat16),
             strip,
             strip,
@@ -446,14 +420,12 @@
             pltpu.VMEM((steps, rows_each, 2 * KC), jnp.bfloat16),
             dma((2, steps)),
             dma((2, steps)),
-            dma((2, steps)),
             dma((2,)),
             dma((2,)),
             dma((bits, steps)),
             dma((bits, steps)),
             dma((2, steps)),
             dma((2, steps)),
-            dma((steps,)),
         ],
         compiler_params=pltpu.CompilerParams(
             collective_id=0, has_side_effects=True, vmem_limit_bytes=38 << 20

time: 52.9 us -> 52.1 us (0.985)
  Pallas kernels: 43.3 us -> 42.5 us
    pallas_call x1, Pallas kernels: 43.3 us -> 42.5 us  [on_device(): pl.pallas_call(step_kernel, in_specs=[in_vmem] * 7, out_specs=in_vmem, ou...]
where the time goes in v6:
time: 52.1 us; the launch traced here: 51.9 us
  Pallas kernels  42.5 us (82%)
  local copies, waits for them, and re-layouts  7.19 us (14%)
  other arithmetic  2.15 us (4%)
    pallas_call x1, Pallas kernels, on_device(): pl.pallas_call(step_kernel, in_specs=[in_vmem] * 7, out_specs=in_vmem, ou...  42.5 us
    unnamed x6, local copies, waits for them, and re-layouts  7.11 us
    sin x2, other arithmetic, angle_parts(): return (jnp.cos(angles), jnp.sin(angles))  1.37 us

profile of v6, /device:TPU:9, one launch (start us, length us, event | category | flops | bytes accessed | tf_op | source)
XLA Modules:
  0.0 51.9 jit_solution(13304411601903010720)
XLA Ops:
  0.0 0.1 pad_add_fusion.2
  0.1 0.7 %pad_add_fusion.1 = s32[64,2]{0,1:T(2,128)S(1)} fusion(s32[64,1]{0,1:T(1,128)} %bitcast.8, s32[64,1]{0,1:T(1,128)} %bitcast.9), kind=kLoop, calls=%fused_computation.23 | loop fusion | flops 128 | bytes 1024 | tf_op jit(solution)/shard_map/stack | solution.py:375
  0.8 0.1 constant_dynamic-slice_fusion
  0.9 0.1 copy.8.bounds
  1.0 0.3 fusion.14
  1.3 1.0 %fusion.6 = (f32[256,136]{1,0:T(8,128)S(1)}, f32[256,136]{1,0:T(8,128)S(1)}) fusion(s32[136]{0:T(256)S(1)} %pad_add_fusion), kind=kLoop, calls=%fused_computation.9 | loop fusion | flops 487424 | bytes 279072 | tf_op jit(solution)/shard_map/sin | solution.py:19
  2.3 0.0 copy-start
  2.4 2.5 %copy-done = f32[5,32,8,1024]{3,2,1,0:T(8,128)S(1)} copy-done((f32[5,32,8,1024]{3,2,1,0:T(8,128)S(1)}, f32[5,32,8,1024]{3,2,1,0:T(8,128)}, u32[]{:S(2)}) %copy-start) | copy-done | bytes 5242904
  4.8 0.0 copy-start.1
  4.8 2.2 %copy-done.1 = f32[4,32,8,1024]{3,2,1,0:T(8,128)S(1)} copy-done((f32[4,32,8,1024]{3,2,1,0:T(8,128)S(1)}, f32[4,32,8,1024]{3,2,1,0:T(8,128)}, u32[]{:S(2)}) %copy-start.1) | copy-done | bytes 4194328
  7.0 42.5 %step.1 = f32[5,256,1024]{2,1,0:T(8,128)S(1)} custom-call(f32[5,256,1024]{2,1,0:T(8,128)S(1)} %bitcast.6, f32[4,256,1024]{2,1,0:T(8,128)S(1)} %bitcast.7, f32[64,256]{1,0:T(8,128)S(1)} %get-tuple-element.8.cosines, f32[64,256]{1,0:T(8,128)S(1)} %get-tuple-element.7.sines, f32[256,136]{1,0:T(8,128)S(1)} %get-tuple-element.6.turned_cosines, ...), custom_call_target="tpu_custom_call" | custom-call | tf_op jit(solution)/shard_map/step/pallas_call | solution.py:399
  49.5 2.4 %copy.10 = f32[5,32,8,1024]{3,2,1,0:T(8,128)} copy(f32[5,32,8,1024]{3,2,1,0:T(8,128)S(1)} %bitcast.5) | data formatting | bytes 10485760
  (5 shorter events, 0.0 us)
Async XLA Ops:
  2.3 2.5 %copy-start = (f32[5,32,8,1024]{3,2,1,0:T(8,128)S(1)}, f32[5,32,8,1024]{3,2,1,0:T(8,128)}, u32[]{:S(2)}) copy-start(f32[5,32,8,1024]{3,2,1,0:T(8,128)} %param.4) | copy-start | bytes 15728644
  4.8 2.2 %copy-start.1 = (f32[4,32,8,1024]{3,2,1,0:T(8,128)S(1)}, f32[4,32,8,1024]{3,2,1,0:T(8,128)}, u32[]{:S(2)}) copy-start(f32[4,32,8,1024]{3,2,1,0:T(8,128)} %param.5) | copy-start | bytes 12582916
